TPU v7x, 32 devices: a whole 2x2x4 slice. The times are simulated.
32 devices in a mesh: groups: 2 (over y), srv: 4 (over z), hid: 2 (over x), rep: 2 (over core).
Axes of the slice: x: 2, y: 2, z: 4, core: 2. Of those that a mesh axis runs over, the one named last changes fastest.
Arguments:
- layer_input: bfloat16 [2048, 4096], P(('groups', 'srv'), ('hid', 'rep')), parts along dimension 0, may hold values from -12 to 12
- query_weight: bfloat16 [4096, 4096], P('srv', ('hid', 'rep')), may hold values from -0.09375 to 0.09375
- key_weight: bfloat16 [4096, 1024], P('srv', ('hid', 'rep')), may hold values from -0.09375 to 0.09375
- value_weight: bfloat16 [4096, 1024], P('srv', ('hid', 'rep')), may hold values from -0.09375 to 0.09375
- out_grad: bfloat16 [2048, 4096], P(('groups', 'srv'), ('hid', 'rep')), parts along dimension 0, may hold values from -6 to 6
- doc_ids: int32 [2048], P('groups'), parts along dimension 0, may hold values from 0 to 7, never falling along the last dimension, each value on 1 to 512 neighbouring positions
Outputs:
- input_grad: bfloat16 [2048, 4096], P(('groups', 'srv'), ('hid', 'rep')), parts along dimension 0
- query_weight_grad: float32 [8192, 4096], P(('groups', 'srv'), ('hid', 'rep')), parts along dimension 0
- key_weight_grad: float32 [8192, 1024], P(('groups', 'srv'), ('hid', 'rep')), parts along dimension 0
- value_weight_grad: float32 [8192, 1024], P(('groups', 'srv'), ('hid', 'rep')), parts along dimension 0
There are 2 independent parts, one for each index of `groups`. A program takes and returns all parts, laid end to end along the dimension named above; an argument that names none is the same for every part. Nothing has to cross between parts.
Inputs may be any that keep to these rules, and one draw needn't show every extreme that they name: `doc_ids`: document numbers never fall along the tokens; every document holds at most 512 tokens and one holds exactly 512.
All inputs are finite; a program needn't handle non-finite values.
Results may differ from a plain program's by a relative error of at most 0.011.
Values may be sent and summed in bfloat16 or wider, within the bound.
A program may use at most 64 MiB of HBM per device.

v0:
```python
import functools

import jax
import jax.numpy as jnp
from jax import lax
from jax.experimental import pallas as pl
from jax.experimental.pallas import tpu as pltpu
from jax.sharding import PartitionSpec as P

HQ = 32
HK = 8
DH = 128
BLOCK = 128


NEGATIVE = -1e30


def attend(queries, cotangent, keys_all, values_all, doc_ids, block_id, carried):
    row_count = queries.shape[0]
    factor_scale = queries.shape[-1] ** (-0.5)
    offsets = jnp.arange(row_count, dtype=jnp.int32)
    query_pos = block_id * row_count + offsets
    query_doc = lax.dynamic_slice_in_dim(doc_ids, block_id * row_count, row_count)
    doc_start = jnp.sum((doc_ids < query_doc[0]).astype(jnp.int32))
    lowest = doc_start // row_count
    highest = jnp.where(True, block_id + 1, lowest)

    def scores_at(key_block):
        key_rows = lax.dynamic_slice_in_dim(keys_all, key_block * row_count, row_count, 0)
        value_rows = lax.dynamic_slice_in_dim(values_all, key_block * row_count, row_count, 0)
        key_doc = lax.dynamic_slice_in_dim(doc_ids, key_block * row_count, row_count)
        key_pos = key_block * row_count + offsets
        allowed = (key_doc[None, :] == query_doc[:, None]) & (
            key_pos[None, :] <= query_pos[:, None]
        )
        logits = (
            jnp.einsum("qgnd,kgd->gnqk", queries, key_rows, preferred_element_type=jnp.float32)
            * factor_scale
        )
        logits = jnp.where(allowed, logits, NEGATIVE)
        slopes = jnp.einsum(
            "qgnd,kgd->gnqk", cotangent, value_rows, preferred_element_type=jnp.float32
        )
        return (key_rows, allowed, logits, slopes)

    def first_pass(key_block, loop_state):
        row_peak, row_total, row_inner = loop_state
        key_rows, allowed, logits, slopes = scores_at(key_block)
        new_peak = jnp.maximum(row_peak, jnp.max(logits, axis=-1))
        weights = jnp.where(allowed, jnp.exp(logits - new_peak[..., None]), 0.0)
        factor = jnp.exp(row_peak - new_peak)
        row_total = row_total * factor + jnp.sum(weights, axis=-1)
        row_inner = row_inner * factor + jnp.sum(weights * slopes, axis=-1)
        return (new_peak, row_total, row_inner)

    stat_shape = (queries.shape[1], queries.shape[2], row_count)
    initial = (
        jnp.full(stat_shape, NEGATIVE, jnp.float32),
        jnp.zeros(stat_shape, jnp.float32),
        jnp.zeros(stat_shape, jnp.float32),
    )
    row_peak, row_total, row_inner = lax.fori_loop(lowest, highest, first_pass, initial)
    safe_total = jnp.where(True, row_total, 1.0)
    row_delta = row_inner / safe_total
    log_total = row_peak + jnp.log(safe_total)

    def second_pass(key_block, loop_state):
        query_grad, key_accum, value_accum = loop_state
        key_rows, allowed, logits, slopes = scores_at(key_block)
        attention = jnp.where(allowed, jnp.exp(logits - log_total[..., None]), 0.0)
        score_grad = (attention * (slopes - row_delta[..., None]) * factor_scale).astype(
            jnp.bfloat16
        )
        value_part = jnp.einsum(
            "gnqk,qgnd->kgd",
            attention.astype(jnp.bfloat16),
            cotangent,
            preferred_element_type=jnp.float32,
        )
        key_part = jnp.einsum(
            "gnqk,qgnd->kgd", score_grad, queries, preferred_element_type=jnp.float32
        )
        query_grad = query_grad + jnp.einsum(
            "gnqk,kgd->qgnd", score_grad, key_rows, preferred_element_type=jnp.float32
        )
        first_row = key_block * row_count
        key_accum = lax.dynamic_update_slice_in_dim(
            key_accum,
            lax.dynamic_slice_in_dim(key_accum, first_row, row_count, 0) + key_part,
            first_row,
            0,
        )
        value_accum = lax.dynamic_update_slice_in_dim(
            value_accum,
            lax.dynamic_slice_in_dim(value_accum, first_row, row_count, 0) + value_part,
            first_row,
            0,
        )
        return (query_grad, key_accum, value_accum)

    start_grad = jnp.zeros(queries.shape, jnp.float32)
    query_grad, key_accum, value_accum = lax.fori_loop(
        lowest, highest, second_pass, (start_grad, carried[0], carried[1])
    )
    return (query_grad, (key_accum, value_accum))


def body(layer_input, query_weight, key_weight, value_weight, out_grad, doc_ids):
    tok_rows = layer_input.shape[0]
    query_width = query_weight.shape[1]
    pair_width = key_weight.shape[1]
    key_heads = pair_width // DH
    group_size = HQ // HK
    block_count = tok_rows // BLOCK
    owner_id = lax.axis_index("srv")
    weights_all = lax.all_gather(
        jnp.concatenate([query_weight, key_weight, value_weight], axis=1), "srv", axis=0, tiled=True
    )
    inputs_all = lax.all_gather(layer_input, ("hid", "rep"), axis=1, tiled=True)
    projected = jnp.dot(inputs_all, weights_all, preferred_element_type=jnp.float32).astype(
        jnp.bfloat16
    )
    queries = projected[:, :query_width].reshape(block_count, BLOCK, key_heads, group_size, DH)
    keys_local = projected[:, query_width : query_width + pair_width]
    values_local = projected[:, query_width + pair_width :]
    keys_all, values_all = (
        lax.all_gather(keys_local, "srv", axis=0, tiled=True),
        lax.all_gather(values_local, "srv", axis=0, tiled=True),
    )
    total_rows = keys_all.shape[0]
    keys_all = keys_all.reshape(total_rows, key_heads, DH)
    values_all = values_all.reshape(total_rows, key_heads, DH)
    cotangent = out_grad.reshape(block_count, BLOCK, key_heads, group_size, DH)
    empty_accum = jnp.zeros((total_rows, key_heads, DH), jnp.float32)

    def own_block(position, loop_state):
        answers, carried = loop_state
        grad_q, carried = attend(
            lax.dynamic_index_in_dim(queries, position, 0, keepdims=False),
            lax.dynamic_index_in_dim(cotangent, position, 0, keepdims=False),
            keys_all,
            values_all,
            doc_ids,
            owner_id * block_count + position,
            carried,
        )
        answers = lax.dynamic_update_index_in_dim(answers, grad_q.astype(jnp.bfloat16), position, 0)
        return (answers, carried)

    answers = jnp.zeros(queries.shape, jnp.bfloat16)
    answers, carried = lax.fori_loop(
        0, block_count, own_block, (answers, (empty_accum, empty_accum))
    )
    query_grad = answers.reshape(tok_rows, query_width)
    key_accum, value_accum = carried
    key_sum, value_sum = (
        lax.psum_scatter(key_accum, "srv", scatter_dimension=0, tiled=True),
        lax.psum_scatter(value_accum, "srv", scatter_dimension=0, tiled=True),
    )
    grads_all = jnp.concatenate(
        [
            query_grad,
            key_sum.astype(jnp.bfloat16).reshape(tok_rows, pair_width),
            value_sum.astype(jnp.bfloat16).reshape(tok_rows, pair_width),
        ],
        axis=1,
    )
    input_terms = lax.dot_general(
        grads_all, weights_all, (((1,), (1,)), ((), ())), preferred_element_type=jnp.float32
    )
    input_grad = lax.psum_scatter(
        input_terms, ("hid", "rep"), scatter_dimension=1, tiled=True
    ).astype(jnp.bfloat16)
    columns = lax.all_to_all(inputs_all, "srv", split_axis=1, concat_axis=0, tiled=True)
    weight_grad = lax.dot_general(
        columns,
        lax.all_gather(grads_all, "srv", axis=0, tiled=True),
        (((0,), (0,)), ((), ())),
        preferred_element_type=jnp.float32,
    )
    return (
        input_grad,
        weight_grad[:, :query_width],
        weight_grad[:, query_width : query_width + pair_width],
        weight_grad[:, query_width + pair_width :],
    )


MESH = pl.DeviceIdType.MESH
VM = pl.BlockSpec(memory_space=pltpu.VMEM)
VMEM_BYTES = 60 * 1024 * 1024


def place(n_rep):
    return lax.axis_index("srv"), lax.axis_index("hid") * n_rep + lax.axis_index("rep")


def device_at(z, c, n_rep):
    return {"srv": z, "hid": c // n_rep, "rep": c % n_rep}


def greet(n, m, n_rep):
    z, c = place(n_rep)
    barrier = pltpu.get_barrier_semaphore()
    for dz in range(n):
        for dc in range(m):
            if dz or dc:
                pl.semaphore_signal(
                    barrier,
                    inc=1,
                    device_id=device_at((z + dz) % n, (c + dc) % m, n_rep),
                    device_id_type=MESH,
                )
    pl.semaphore_wait(barrier, n * m - 1)


def remote(src, dst, send, recv, device):
    return pltpu.make_async_remote_copy(
        src_ref=src, dst_ref=dst, send_sem=send, recv_sem=recv, device_id=device, device_id_type=MESH
    )


def rows_at(start, size):
    return pl.ds(pl.multiple_of(start, size), size)


def project_kernel(
    n, m, n_rep, share,
    x_ref, og_ref, qw_ref, kw_ref, vw_ref,
    cols_ref, og_out, qkv_ref,
    part, took, relay,
    og_send, og_recv, a_send, a_recv, b_send, b_recv, c_send, c_recv, v_send, v_recv, own_sem,
):
    z, c = place(n_rep)
    tok = x_ref.shape[0]
    piece = tok // m
    q_cols = qw_ref.shape[1] // n
    half, odd = z // 2, z % 2
    partner = z + 1 - 2 * odd
    middle = half != odd
    far = 2 * (1 - half)
    kv_cols = rows_at(q_cols + odd * DH, DH)
    greet(n, m, n_rep)

    own = c == z
    for dq in range(m):
        q = (c + dq) % m
        src = x_ref.at[rows_at(q * piece, piece)]
        dst = cols_ref.at[rows_at(z * tok + q * piece, piece)]
        if dq == 0:
            @pl.when(own)
            def _():
                pltpu.make_async_copy(src, dst, a_recv.at[z]).start()

            @pl.when(jnp.logical_not(own))
            def _():
                remote(src, dst, a_send.at[dq], a_recv.at[z], device_at(c, q, n_rep)).start()
        else:
            remote(src, dst, a_send.at[dq], a_recv.at[z], device_at(c, q, n_rep)).start()
    og_dst = og_out.at[rows_at(z * tok, tok)]
    og_copies = []
    for d in range(1, n):
        to = (z + d) % n
        copy = remote(
            og_ref.at[:, rows_at(to * q_cols, q_cols)], og_dst,
            og_send.at[d], og_recv.at[d], device_at(to, c, n_rep),
        )
        copy.start()
        og_copies.append(copy)
    og_own = pltpu.make_async_copy(og_ref.at[:, rows_at(z * q_cols, q_cols)], og_dst, own_sem)
    og_own.start()

    def spread_copy(t, d):
        block = cols_ref.at[rows_at(t * tok + c * piece, piece)]
        return remote(
            block, block, b_send.at[t, d], b_recv.at[t, d], device_at(z, (c + d) % m, n_rep)
        )

    def part_copy(t, slot):
        rows = rows_at(t * tok, tok)
        src = part.at[partner if slot == 0 else far + slot - 1, rows]
        dst = took.at[0, rows] if slot == 0 else relay.at[slot - 1, rows]
        return remote(
            src, dst, c_send.at[t, slot], c_recv.at[t, slot], device_at(partner, c, n_rep)
        )

    def far_copy(t, slot):
        to = far + slot - 1
        rows = rows_at(t * tok, tok)
        return remote(
            part.at[to, rows], took.at[1, rows],
            c_send.at[t, slot], c_recv.at[t, 3], device_at(to, c, n_rep),
        )

    def swap_copy(t):
        block = qkv_ref.at[rows_at(t * tok, tok), kv_cols]
        return remote(block, block, v_send.at[t], v_recv.at[t], device_at(partner, c, n_rep))

    def pass_on(t):
        rows = rows_at(t * tok, tok)

        @pl.when(middle)
        def _():
            for slot in (1, 2):
                part_copy(t, slot).wait_recv()
                to = far + slot - 1
                total = part[to, rows, :].astype(jnp.float32)
                total = total + relay[slot - 1, rows, :].astype(jnp.float32)
                part[to, rows, :] = total.astype(jnp.bfloat16)
                far_copy(t, slot).start()

    def spread(i, carry):
        t = (2 * half + i) % n
        block = cols_ref.at[rows_at(t * tok + c * piece, piece)]
        pltpu.make_async_copy(block, block, a_recv.at[t]).wait()
        for d in range(1, m):
            spread_copy(t, d).start()
        return carry

    lax.fori_loop(0, n, spread, 0)

    def multiply(i, carry):
        t = (2 * half + i) % n
        for d in range(1, m):
            spread_copy(t, d).wait_recv()
        rows = rows_at(t * tok, tok)
        x = cols_ref[rows, :]
        keys = jnp.dot(x, kw_ref[...], preferred_element_type=jnp.float32).astype(jnp.bfloat16)
        values = jnp.dot(x, vw_ref[...], preferred_element_type=jnp.float32).astype(jnp.bfloat16)
        for s in range(n):
            j = s // share
            part[s, rows, :q_cols] = jnp.dot(
                x, qw_ref[:, s * q_cols : (s + 1) * q_cols], preferred_element_type=jnp.float32
            ).astype(jnp.bfloat16)
            pair = values if s % 2 else keys
            part[s, rows, q_cols:] = pair[:, j * DH : (j + 1) * DH]

        @pl.when(jnp.logical_not(middle))
        def _():
            for slot in (1, 2):
                part_copy(t, slot).start()

        part_copy(t, 0).start()

        @pl.when(i > 0)
        def _():
            pass_on((2 * half + i - 1) % n)

        return carry

    lax.fori_loop(0, n, multiply, 0)
    pass_on((2 * half + n - 1) % n)

    def collect(i, carry):
        t = (2 * half + i) % n
        rows = rows_at(t * tok, tok)
        part_copy(t, 0).wait_recv()
        pltpu.make_async_copy(took.at[1, rows], took.at[1, rows], c_recv.at[t, 3]).wait()
        total = part[z, rows, :].astype(jnp.float32)
        for slot in range(2):
            total = total + took[slot, rows, :].astype(jnp.float32)
        total = total.astype(jnp.bfloat16)
        qkv_ref[rows, :q_cols] = total[:, :q_cols]
        qkv_ref[rows, kv_cols] = total[:, q_cols:]
        swap_copy(t).start()
        return carry

    lax.fori_loop(0, n, collect, 0)

    def drain(t, carry):
        for d in range(1, m):
            spread_copy(t, d).wait_send()
        for slot in range(3):
            part_copy(t, slot).wait_send()
        swap_copy(t).wait()
        return carry

    lax.fori_loop(0, n, drain, 0)
    og_own.wait()
    for copy in og_copies:
        copy.wait()
    for dq in range(m):
        q = (c + dq) % m
        src = x_ref.at[rows_at(q * piece, piece)]
        dst = cols_ref.at[rows_at(z * tok + q * piece, piece)]
        copy = remote(src, dst, a_send.at[dq], a_recv.at[z], device_at(c, q, n_rep))
        if dq == 0:
            @pl.when(jnp.logical_not(own))
            def _():
                copy.wait_send()
        else:
            copy.wait_send()


def attend_kernel(longest, row_block, qkv_ref, og_ref, dr_ref, dc_ref, dq_ref, mine_ref, give_ref, dk, dv):
    total_rows = qkv_ref.shape[0]
    q_cols = og_ref.shape[1]
    heads = q_cols // DH
    scale = DH ** (-0.5)
    dk[...] = jnp.zeros_like(dk)
    dv[...] = jnp.zeros_like(dv)
    for first in range(0, total_rows, row_block):
        last = first + row_block
        low = max(0, (first + 1 - longest) // 128 * 128)
        width = last - low
        queries = jnp.concatenate(
            [qkv_ref[first:last, h * DH : (h + 1) * DH] for h in range(heads)], axis=0
        )
        cotangent = jnp.concatenate(
            [og_ref[first:last, h * DH : (h + 1) * DH] for h in range(heads)], axis=0
        )
        keys = qkv_ref[low:last, q_cols : q_cols + DH]
        values = qkv_ref[low:last, q_cols + DH :]
        row_pos = first + lax.broadcasted_iota(jnp.int32, (row_block, width), 0)
        key_pos = low + lax.broadcasted_iota(jnp.int32, (row_block, width), 1)
        kept = (dr_ref[first:last, :] == dc_ref[:, low:last]) & (key_pos <= row_pos)
        allowed = jnp.concatenate([jnp.where(kept, 1.0, 0.0)] * heads, axis=0) > 0.5
        both = (((1,), (1,)), ((), ()))
        logits = lax.dot_general(queries, keys, both, preferred_element_type=jnp.float32) * scale
        logits = jnp.where(allowed, logits, NEGATIVE)
        weights = jnp.where(allowed, jnp.exp(logits - jnp.max(logits, axis=1, keepdims=True)), 0.0)
        attention = weights / jnp.sum(weights, axis=1, keepdims=True)
        slopes = lax.dot_general(cotangent, values, both, preferred_element_type=jnp.float32)
        inner = jnp.sum(attention * slopes, axis=1, keepdims=True)
        score_grad = (attention * (slopes - inner) * scale).astype(jnp.bfloat16)
        down = (((0,), (0,)), ((), ()))
        query_grad = jnp.dot(score_grad, keys, preferred_element_type=jnp.float32)
        for h in range(heads):
            dq_ref[first:last, h * DH : (h + 1) * DH] = query_grad[
                h * row_block : (h + 1) * row_block
            ].astype(jnp.bfloat16)
        dk[low:last, :] += lax.dot_general(
            score_grad, queries, down, preferred_element_type=jnp.float32
        )
        dv[low:last, :] += lax.dot_general(
            attention.astype(jnp.bfloat16), cotangent, down, preferred_element_type=jnp.float32
        )
    odd = lax.axis_index("srv") % 2 == 1

    @pl.when(odd)
    def _():
        mine_ref[...] = dv[...]
        give_ref[...] = dk[...].astype(jnp.bfloat16)

    @pl.when(jnp.logical_not(odd))
    def _():
        mine_ref[...] = dk[...]
        give_ref[...] = dv[...].astype(jnp.bfloat16)


def spread_kernel(
    n, m, n_rep,
    dq_ref, mine_ref, give_ref, qw_ref, kw_ref, vw_ref,
    dqa_ref, kva_ref, ig_ref,
    pair, stage, terms, took, done,
    p_send, p_recv, q_send, q_recv, k_send, k_recv, r_send, r_recv, e_send, e_recv,
):
    z, c = place(n_rep)
    tok, _ = ig_ref.shape
    piece = tok // m
    q_cols = dq_ref.shape[1]
    greet(n, m, n_rep)
    half, odd = z // 2, z % 2
    partner = z + 1 - 2 * odd
    middle = half != odd
    far = 2 * (1 - half)
    near = 2 - half
    pair_copy = remote(give_ref, pair, p_send, p_recv, device_at(partner, c, n_rep))
    pair_copy.start()
    my_cols = rows_at(z * q_cols, q_cols)
    my_head = rows_at(half * DH, DH)

    def query_copy(t, slot):
        rows = rows_at(t * tok, tok)
        owner = z if slot < 2 else far + slot - 2
        there = dqa_ref.at[rows, rows_at(owner * q_cols, q_cols)]
        return remote(
            dq_ref.at[rows] if slot < 2 else there, there,
            q_send.at[t, slot], q_recv.at[t, owner],
            device_at(near if slot == 1 else partner, c, n_rep),
        )

    def pair_out(t, slot):
        rows = rows_at(t * tok, tok)
        owner = z if slot < 2 else far + slot - 2
        there = kva_ref.at[owner % 2, rows, rows_at(owner // 2 * DH, DH)]
        return remote(
            stage.at[rows] if slot < 2 else there, there,
            k_send.at[t, slot], k_recv.at[t, owner],
            device_at(near if slot == 1 else partner, c, n_rep),
        )

    def await_owner(t, owner):
        rows = rows_at(t * tok, tok)
        block = dqa_ref.at[rows, rows_at(owner * q_cols, q_cols)]
        pltpu.make_async_copy(block, block, q_recv.at[t, owner]).wait()

    def await_pair(t, owner):
        rows = rows_at(t * tok, tok)
        block = kva_ref.at[owner % 2, rows, rows_at(owner // 2 * DH, DH)]
        pltpu.make_async_copy(block, block, k_recv.at[t, owner]).wait()

    def term_copy(t, d):
        to = (c + d) % m
        return remote(
            terms.at[rows_at(t * tok + to * piece, piece)],
            took.at[d - 1, rows_at(t * piece, piece)],
            r_send.at[t, d], r_recv.at[t, d], device_at(z, to, n_rep),
        )

    def done_copy(t):
        return remote(
            done.at[rows_at(t * piece, piece)], ig_ref.at[rows_at(c * piece, piece)],
            e_send.at[t], e_recv.at[c], device_at(t, z, n_rep),
        )

    for slot in (1, 0):
        query_copy(0, slot).start()
    dqa_ref[:, my_cols] = dq_ref[...]
    pair_copy.wait()
    summed = (mine_ref[...] + pair[...].astype(jnp.float32)).astype(jnp.bfloat16)
    stage[...] = summed
    kva_ref[odd, :, my_head] = summed
    for slot in (1, 0):
        pair_out(0, slot).start()

    def send_chunk(t, carry):
        for slot in (1, 0):
            query_copy(t, slot).start()
            pair_out(t, slot).start()
        return carry

    lax.fori_loop(1, n, send_chunk, 0)

    def finish(t):
        for d in range(1, m):
            term_copy(t, d).wait_recv()
        total = terms[rows_at(t * tok + c * piece, piece), :].astype(jnp.float32)
        for d in range(1, m):
            total = total + took[d - 1, rows_at(t * piece, piece), :].astype(jnp.float32)
        done[rows_at(t * piece, piece), :] = total.astype(jnp.bfloat16)
        own = (t == z) & (c == z)

        @pl.when(own)
        def _():
            pltpu.make_async_copy(
                done.at[rows_at(t * piece, piece)],
                ig_ref.at[rows_at(c * piece, piece)],
                e_recv.at[c],
            ).start()

        @pl.when(jnp.logical_not(own))
        def _():
            done_copy(t).start()

    def chunk(t, carry):
        rows = rows_at(t * tok, tok)
        for slot in (2, 3):
            await_owner(t, far + slot - 2)

            @pl.when(middle)
            def _():
                query_copy(t, slot).start()

        for slot in (2, 3):
            await_pair(t, far + slot - 2)

            @pl.when(middle)
            def _():
                pair_out(t, slot).start()

        await_owner(t, partner)
        await_pair(t, partner)
        across = (((1,), (1,)), ((), ()))
        total = lax.dot_general(
            dqa_ref[rows, :], qw_ref[...], across, preferred_element_type=jnp.float32
        )
        total = total + lax.dot_general(
            kva_ref[0, rows, :], kw_ref[...], across, preferred_element_type=jnp.float32
        )
        total = total + lax.dot_general(
            kva_ref[1, rows, :], vw_ref[...], across, preferred_element_type=jnp.float32
        )
        terms[rows, :] = total.astype(jnp.bfloat16)
        for d in range(1, m):
            term_copy(t, d).start()

        @pl.when(t > 0)
        def _():
            finish(t - 1)

        return carry

    lax.fori_loop(0, n, chunk, 0)
    finish(jnp.int32(n - 1))

    def drain(t, carry):
        for slot in (0, 1):
            query_copy(t, slot).wait_send()
            pair_out(t, slot).wait_send()

        @pl.when(middle)
        def _():
            for slot in (2, 3):
                query_copy(t, slot).wait_send()
                pair_out(t, slot).wait_send()

        for d in range(1, m):
            term_copy(t, d).wait_send()

        @pl.when(jnp.logical_not((t == z) & (c == z)))
        def _():
            done_copy(t).wait_send()

        return carry

    lax.fori_loop(0, n, drain, 0)
    for q in range(m):
        block = ig_ref.at[q * piece : (q + 1) * piece]
        pltpu.make_async_copy(block, block, e_recv.at[q]).wait()


def stationary(n, n_hid, n_rep, layer_input, query_weight, key_weight, value_weight, out_grad, doc_ids):
    m = n_hid * n_rep
    bf16, f32 = jnp.bfloat16, jnp.float32
    tok, feats = layer_input.shape
    total = tok * n
    q_cols = query_weight.shape[1] // n
    pair_width = key_weight.shape[1]
    share = n // (pair_width // DH)
    width = q_cols + 2 * DH
    dma = pltpu.SemaphoreType.DMA
    columns, cotangent, qkv = pl.pallas_call(
        functools.partial(project_kernel, n, m, n_rep, share),
        out_shape=(
            jax.ShapeDtypeStruct((total, feats), bf16),
            jax.ShapeDtypeStruct((total, q_cols), bf16),
            jax.ShapeDtypeStruct((total, width), bf16),
        ),
        in_specs=[VM] * 5,
        out_specs=(VM,) * 3,
        scratch_shapes=[
            pltpu.VMEM((n, total, q_cols + DH), bf16),
            pltpu.VMEM((2, total, q_cols + DH), bf16),
            pltpu.VMEM((2, total, q_cols + DH), bf16),
            dma((n,)), dma((n,)), dma((m,)), dma((n,)),
            dma((n, m)), dma((n, m)), dma((n, 3)), dma((n, 4)), dma((n,)), dma((n,)), dma,
        ],
        compiler_params=pltpu.CompilerParams(
            collective_id=0, has_side_effects=True, vmem_limit_bytes=VMEM_BYTES
        ),
    )(layer_input, out_grad, query_weight, key_weight, value_weight)
    query_grad, mine, give = pl.pallas_call(
        functools.partial(attend_kernel, total // 2, BLOCK),
        out_shape=(
            jax.ShapeDtypeStruct((total, q_cols), bf16),
            jax.ShapeDtypeStruct((total, DH), f32),
            jax.ShapeDtypeStruct((total, DH), bf16),
        ),
        in_specs=[VM] * 4,
        out_specs=(VM,) * 3,
        scratch_shapes=[pltpu.VMEM((total, DH), f32), pltpu.VMEM((total, DH), f32)],
        compiler_params=pltpu.CompilerParams(vmem_limit_bytes=VMEM_BYTES),
    )(qkv, cotangent, doc_ids.reshape(total, 1), doc_ids.reshape(1, total))
    queries_all, pairs_all, input_grad = pl.pallas_call(
        functools.partial(spread_kernel, n, m, n_rep),
        out_shape=(
            jax.ShapeDtypeStruct((total, q_cols * n), bf16),
            jax.ShapeDtypeStruct((2, total, pair_width), bf16),
            jax.ShapeDtypeStruct((tok, feats), bf16),
        ),
        in_specs=[VM] * 6,
        out_specs=(VM,) * 3,
        scratch_shapes=[
            pltpu.VMEM((total, DH), bf16),
            pltpu.VMEM((total, DH), bf16),
            pltpu.VMEM((total, feats), bf16),
            pltpu.VMEM((m - 1, tok // m * n, feats), bf16),
            pltpu.VMEM((tok // m * n, feats), bf16),
            dma, dma, dma((n, n)), dma((n, n)), dma((n, n)), dma((n, n)),
            dma((n, m)), dma((n, m)), dma((n,)), dma((m,)),
        ],
        compiler_params=pltpu.CompilerParams(
            collective_id=1, has_side_effects=True, vmem_limit_bytes=VMEM_BYTES
        ),
    )(query_grad, mine, give, query_weight, key_weight, value_weight)

    def weight_grad(grads):
        return lax.dot_general(
            columns, grads, (((0,), (0,)), ((), ())), preferred_element_type=f32
        )

    return (
        input_grad,
        weight_grad(queries_all),
        weight_grad(pairs_all[0]),
        weight_grad(pairs_all[1]),
    )


def solution(mesh):
    in_specs = (
        P(("groups", "srv"), ("hid", "rep")),
        P("srv", ("hid", "rep")),
        P("srv", ("hid", "rep")),
        P("srv", ("hid", "rep")),
        P(("groups", "srv"), ("hid", "rep")),
        P("groups"),
    )
    out_specs = (
        P(("groups", "srv"), ("hid", "rep")),
        P(("groups", "srv"), ("hid", "rep")),
        P(("groups", "srv"), ("hid", "rep")),
        P(("groups", "srv"), ("hid", "rep")),
    )
    n, n_hid, n_rep = mesh.shape["srv"], mesh.shape["hid"], mesh.shape["rep"]
    m = n_hid * n_rep
    inner = body
    if n == m and HK % m == 0 and 2 * (HK // m) == n and (HQ // m) % n == 0:
        inner = functools.partial(stationary, n, n_hid, n_rep)
    return jax.shard_map(inner, mesh=mesh, in_specs=in_specs, out_specs=out_specs, check_vma=False)
```

profile of v0, /device:TPU:0, one launch (start us, length us, event | category | flops | bytes accessed | tf_op | source)
XLA Modules:
  0.0 202.3 jit_solution(7425564315647580804)
XLA Ops:
  0.6 0.0 copy-start.1
  0.6 94.1 %shard_map.93 = (bf16[1024,1024]{1,0:T(8,128)(2,1)}, bf16[1024,256]{1,0:T(8,128)(2,1)}, bf16[1024,512]{1,0:T(8,128)(2,1)}) custom-call(bf16[256,1024]{1,0:T(8,128)(2,1)} %x_ref.1, bf16[256,1024]{1,0:T(8,128)(2,1)} %og_ref.1, bf16[1024,1024]{1,0:T(8,128)(2,1)} %qw_ref.3, bf16[1024,256]{1,0:T(8,128)(2,1)} %kw_ref.3, bf16[1024,256]{1,0:T(8,128)(2,1)} %vw_ref.3), custom_call_target="tpu_custom_call" | custom-call | tf_op jit(solution)/shard_map/pallas_call | solution.py:634
  94.8 0.0 copy-done.1
  94.8 1.0 copy.10.dr_ref
  95.8 8.6 %shard_map.94 = (bf16[1024,256]{1,0:T(8,128)(2,1)}, f32[1024,128]{1,0:T(8,128)}, bf16[1024,128]{1,0:T(8,128)(2,1)}) custom-call(bf16[1024,512]{1,0:T(8,128)(2,1)} %get-tuple-element.13.qkv_ref, bf16[1024,256]{1,0:T(8,128)(2,1)} %get-tuple-element.14.og_ref, s32[1024,1]{1,0:T(8,128)} %copy.10.dr_ref, s32[1,1024]{1,0:T(1,128)} %bitcast.12), custom_call_target="tpu_custom_call" | custom-call | tf_op jit(solution)/shard_map/pallas_call | solution.py:654
  104.4 0.0 copy-start.2
  104.4 87.5 %shard_map.95 = (bf16[1024,1024]{1,0:T(8,128)(2,1)}, bf16[2,1024,256]{2,1,0:T(8,128)(2,1)}, bf16[256,1024]{1,0:T(8,128)(2,1)}) custom-call(bf16[1024,256]{1,0:T(8,128)(2,1)} %get-tuple-element.15.dq_ref, f32[1024,128]{1,0:T(8,128)} %get-tuple-element.16.mine_ref, bf16[1024,128]{1,0:T(8,128)(2,1)} %get-tuple-element.17.give_ref, bf16[1024,1024]{1,0:T(8,128)(2,1)} %qw_ref.3, ...), custom_call_target="tpu_custom_call" | custom-call | tf_op jit(solution)/shard_map/pallas_call | solution.py:666
  191.9 0.0 copy-done.2
  191.9 0.0 copy-start.3
  191.9 6.1 %fusion.6 = f32[1024,1024]{1,0:T(8,128)} fusion(bf16[1024,1024]{1,0:T(8,128)(2,1)S(1)} %copy-done.2, bf16[1024,1024]{1,0:T(8,128)(2,1)} %get-tuple-element.20), kind=kOutput, calls=%fused_computation.6 | convolution fusion | flops 2147483648 | bytes 8388608 | tf_op jit(solution)/shard_map/dot_general | solution.py:690
  198.0 0.0 copy-done.3
  198.0 1.7 fusion.2
  199.7 0.0 copy-start
  199.7 1.7 fusion
  201.5 0.0 copy-done
  201.5 0.8 copy.12
Async XLA Ops:
  0.6 94.1 %copy-start.1 = (s32[1024]{0:T(1024)S(1)}, s32[1024]{0:T(1024)}, u32[]{:S(2)}) copy-start(s32[1024]{0:T(1024)} %param.11) | copy-start | bytes 12292
  104.4 87.5 %copy-start.2 = (bf16[1024,1024]{1,0:T(8,128)(2,1)S(1)}, bf16[1024,1024]{1,0:T(8,128)(2,1)}, u32[]{:S(2)}) copy-start(bf16[1024,1024]{1,0:T(8,128)(2,1)} %get-tuple-element.19) | copy-start | bytes 6291460
  191.9 6.1 %copy-start.3 = (bf16[2,1024,256]{2,1,0:T(8,128)(2,1)S(1)}, bf16[2,1024,256]{2,1,0:T(8,128)(2,1)}, u32[]{:S(2)}) copy-start(bf16[2,1024,256]{2,1,0:T(8,128)(2,1)} %get-tuple-element.21) | copy-start | bytes 3145732
  199.7 1.7 copy-start
where the time goes:
time: 203 us; the launch traced here: 202 us
  Pallas kernels  190 us (94%)
  matrix products  9.5 us (5%)
    pallas_call x1, Pallas kernels, stationary(): pl.pallas_call(functools.partial(project_kernel, n, m, n_rep, share), out...  94.1 us
    pallas_call x1, Pallas kernels, stationary(): pl.pallas_call(functools.partial(spread_kernel, n, m, n_rep), out_shape=(...  87.5 us
    dot_general x3, matrix products, weight_grad(): lax.dot_general(columns, grads, (((0,), (0,)), ((), ())), preferred_eleme...  9.5 us
    pallas_call x1, Pallas kernels, stationary(): pl.pallas_call(functools.partial(attend_kernel, total // 2, BLOCK), out_s...  8.6 us

commit v1 on v0

v1 whole, which is shorter than its diff:
```python
import functools

import jax
import jax.numpy as jnp
from jax import lax
from jax.experimental import pallas as pl
from jax.experimental.pallas import tpu as pltpu
from jax.sharding import PartitionSpec as P

HQ = 32
HK = 8
DH = 128
BLOCK = 128


NEGATIVE = -1e30


def attend(queries, cotangent, keys_all, values_all, doc_ids, block_id, carried):
    row_count = queries.shape[0]
    factor_scale = queries.shape[-1] ** (-0.5)
    offsets = jnp.arange(row_count, dtype=jnp.int32)
    query_pos = block_id * row_count + offsets
    query_doc = lax.dynamic_slice_in_dim(doc_ids, block_id * row_count, row_count)
    doc_start = jnp.sum((doc_ids < query_doc[0]).astype(jnp.int32))
    lowest = doc_start // row_count
    highest = jnp.where(True, block_id + 1, lowest)

    def scores_at(key_block):
        key_rows = lax.dynamic_slice_in_dim(keys_all, key_block * row_count, row_count, 0)
        value_rows = lax.dynamic_slice_in_dim(values_all, key_block * row_count, row_count, 0)
        key_doc = lax.dynamic_slice_in_dim(doc_ids, key_block * row_count, row_count)
        key_pos = key_block * row_count + offsets
        allowed = (key_doc[None, :] == query_doc[:, None]) & (
            key_pos[None, :] <= query_pos[:, None]
        )
        logits = (
            jnp.einsum("qgnd,kgd->gnqk", queries, key_rows, preferred_element_type=jnp.float32)
            * factor_scale
        )
        logits = jnp.where(allowed, logits, NEGATIVE)
        slopes = jnp.einsum(
            "qgnd,kgd->gnqk", cotangent, value_rows, preferred_element_type=jnp.float32
        )
        return (key_rows, allowed, logits, slopes)

    def first_pass(key_block, loop_state):
        row_peak, row_total, row_inner = loop_state
        key_rows, allowed, logits, slopes = scores_at(key_block)
        new_peak = jnp.maximum(row_peak, jnp.max(logits, axis=-1))
        weights = jnp.where(allowed, jnp.exp(logits - new_peak[..., None]), 0.0)
        factor = jnp.exp(row_peak - new_peak)
        row_total = row_total * factor + jnp.sum(weights, axis=-1)
        row_inner = row_inner * factor + jnp.sum(weights * slopes, axis=-1)
        return (new_peak, row_total, row_inner)

    stat_shape = (queries.shape[1], queries.shape[2], row_count)
    initial = (
        jnp.full(stat_shape, NEGATIVE, jnp.float32),
        jnp.zeros(stat_shape, jnp.float32),
        jnp.zeros(stat_shape, jnp.float32),
    )
    row_peak, row_total, row_inner = lax.fori_loop(lowest, highest, first_pass, initial)
    safe_total = jnp.where(True, row_total, 1.0)
    row_delta = row_inner / safe_total
    log_total = row_peak + jnp.log(safe_total)

    def second_pass(key_block, loop_state):
        query_grad, key_accum, value_accum = loop_state
        key_rows, allowed, logits, slopes = scores_at(key_block)
        attention = jnp.where(allowed, jnp.exp(logits - log_total[..., None]), 0.0)
        score_grad = (attention * (slopes - row_delta[..., None]) * factor_scale).astype(
            jnp.bfloat16
        )
        value_part = jnp.einsum(
            "gnqk,qgnd->kgd",
            attention.astype(jnp.bfloat16),
            cotangent,
            preferred_element_type=jnp.float32,
        )
        key_part = jnp.einsum(
            "gnqk,qgnd->kgd", score_grad, queries, preferred_element_type=jnp.float32
        )
        query_grad = query_grad + jnp.einsum(
            "gnqk,kgd->qgnd", score_grad, key_rows, preferred_element_type=jnp.float32
        )
        first_row = key_block * row_count
        key_accum = lax.dynamic_update_slice_in_dim(
            key_accum,
            lax.dynamic_slice_in_dim(key_accum, first_row, row_count, 0) + key_part,
            first_row,
            0,
        )
        value_accum = lax.dynamic_update_slice_in_dim(
            value_accum,
            lax.dynamic_slice_in_dim(value_accum, first_row, row_count, 0) + value_part,
            first_row,
            0,
        )
        return (query_grad, key_accum, value_accum)

    start_grad = jnp.zeros(queries.shape, jnp.float32)
    query_grad, key_accum, value_accum = lax.fori_loop(
        lowest, highest, second_pass, (start_grad, carried[0], carried[1])
    )
    return (query_grad, (key_accum, value_accum))


def body(layer_input, query_weight, key_weight, value_weight, out_grad, doc_ids):
    tok_rows = layer_input.shape[0]
    query_width = query_weight.shape[1]
    pair_width = key_weight.shape[1]
    key_heads = pair_width // DH
    group_size = HQ // HK
    block_count = tok_rows // BLOCK
    owner_id = lax.axis_index("srv")
    weights_all = lax.all_gather(
        jnp.concatenate([query_weight, key_weight, value_weight], axis=1), "srv", axis=0, tiled=True
    )
    inputs_all = lax.all_gather(layer_input, ("hid", "rep"), axis=1, tiled=True)
    projected = jnp.dot(inputs_all, weights_all, preferred_element_type=jnp.float32).astype(
        jnp.bfloat16
    )
    queries = projected[:, :query_width].reshape(block_count, BLOCK, key_heads, group_size, DH)
    keys_local = projected[:, query_width : query_width + pair_width]
    values_local = projected[:, query_width + pair_width :]
    keys_all, values_all = (
        lax.all_gather(keys_local, "srv", axis=0, tiled=True),
        lax.all_gather(values_local, "srv", axis=0, tiled=True),
    )
    total_rows = keys_all.shape[0]
    keys_all = keys_all.reshape(total_rows, key_heads, DH)
    values_all = values_all.reshape(total_rows, key_heads, DH)
    cotangent = out_grad.reshape(block_count, BLOCK, key_heads, group_size, DH)
    empty_accum = jnp.zeros((total_rows, key_heads, DH), jnp.float32)

    def own_block(position, loop_state):
        answers, carried = loop_state
        grad_q, carried = attend(
            lax.dynamic_index_in_dim(queries, position, 0, keepdims=False),
            lax.dynamic_index_in_dim(cotangent, position, 0, keepdims=False),
            keys_all,
            values_all,
            doc_ids,
            owner_id * block_count + position,
            carried,
        )
        answers = lax.dynamic_update_index_in_dim(answers, grad_q.astype(jnp.bfloat16), position, 0)
        return (answers, carried)

    answers = jnp.zeros(queries.shape, jnp.bfloat16)
    answers, carried = lax.fori_loop(
        0, block_count, own_block, (answers, (empty_accum, empty_accum))
    )
    query_grad = answers.reshape(tok_rows, query_width)
    key_accum, value_accum = carried
    key_sum, value_sum = (
        lax.psum_scatter(key_accum, "srv", scatter_dimension=0, tiled=True),
        lax.psum_scatter(value_accum, "srv", scatter_dimension=0, tiled=True),
    )
    grads_all = jnp.concatenate(
        [
            query_grad,
            key_sum.astype(jnp.bfloat16).reshape(tok_rows, pair_width),
            value_sum.astype(jnp.bfloat16).reshape(tok_rows, pair_width),
        ],
        axis=1,
    )
    input_terms = lax.dot_general(
        grads_all, weights_all, (((1,), (1,)), ((), ())), preferred_element_type=jnp.float32
    )
    input_grad = lax.psum_scatter(
        input_terms, ("hid", "rep"), scatter_dimension=1, tiled=True
    ).astype(jnp.bfloat16)
    columns = lax.all_to_all(inputs_all, "srv", split_axis=1, concat_axis=0, tiled=True)
    weight_grad = lax.dot_general(
        columns,
        lax.all_gather(grads_all, "srv", axis=0, tiled=True),
        (((0,), (0,)), ((), ())),
        preferred_element_type=jnp.float32,
    )
    return (
        input_grad,
        weight_grad[:, :query_width],
        weight_grad[:, query_width : query_width + pair_width],
        weight_grad[:, query_width + pair_width :],
    )


MESH = pl.DeviceIdType.MESH
VM = pl.BlockSpec(memory_space=pltpu.VMEM)
VMEM_BYTES = 60 * 1024 * 1024


def place(n_rep):
    return lax.axis_index("srv"), lax.axis_index("hid") * n_rep + lax.axis_index("rep")


def device_at(z, c, n_rep):
    return {"srv": z, "hid": c // n_rep, "rep": c % n_rep}


def greet(n, m, n_rep):
    z, c = place(n_rep)
    barrier = pltpu.get_barrier_semaphore()
    for dz in range(n):
        for dc in range(m):
            if dz or dc:
                pl.semaphore_signal(
                    barrier,
                    inc=1,
                    device_id=device_at((z + dz) % n, (c + dc) % m, n_rep),
                    device_id_type=MESH,
                )
    pl.semaphore_wait(barrier, n * m - 1)


def remote(src, dst, send, recv, device):
    return pltpu.make_async_remote_copy(
        src_ref=src, dst_ref=dst, send_sem=send, recv_sem=recv, device_id=device, device_id_type=MESH
    )


def rows_at(start, size):
    return pl.ds(pl.multiple_of(start, size), size)


def cols_at(start, size):
    return pl.ds(pl.multiple_of(start, DH), size)


def attend_rows(heads, qkv, og_ref, dr_ref, dc_ref, dq_ref, dq_cols, dk, dv, first, row_block, low, width):
    q_cols = heads * DH
    scale = DH ** (-0.5)
    rows = rows_at(first, row_block)
    span = rows_at(low, row_block) if width == row_block else pl.ds(pl.multiple_of(low, row_block), width)
    queries = jnp.concatenate([qkv[rows, h * DH : (h + 1) * DH] for h in range(heads)], axis=0)
    cotangent = jnp.concatenate([og_ref[rows, h * DH : (h + 1) * DH] for h in range(heads)], axis=0)
    keys = qkv[span, q_cols : q_cols + DH]
    values = qkv[span, q_cols + DH : q_cols + 2 * DH]
    row_pos = first + lax.broadcasted_iota(jnp.int32, (row_block, width), 0)
    key_pos = low + lax.broadcasted_iota(jnp.int32, (row_block, width), 1)
    kept = (dr_ref[rows, :] == dc_ref[:, span]) & (key_pos <= row_pos)
    bias = jnp.concatenate([jnp.where(kept, 0.0, NEGATIVE)] * heads, axis=0)
    both = (((1,), (1,)), ((), ()))
    logits = lax.dot_general(queries, keys, both, preferred_element_type=jnp.float32) * scale + bias
    weights = jnp.exp(logits - jnp.max(logits, axis=1, keepdims=True))
    attention = weights * (1.0 / jnp.sum(weights, axis=1, keepdims=True))
    slopes = lax.dot_general(cotangent, values, both, preferred_element_type=jnp.float32)
    inner = jnp.sum(attention * slopes, axis=1, keepdims=True)
    score_grad = (attention * (slopes - inner) * scale).astype(jnp.bfloat16)
    down = (((0,), (0,)), ((), ()))
    query_grad = jnp.dot(score_grad, keys, preferred_element_type=jnp.float32).astype(jnp.bfloat16)
    for h in range(heads):
        dq_ref[rows, cols_at(dq_cols + h * DH, DH)] = query_grad[h * row_block : (h + 1) * row_block]
    dk[span, :] += lax.dot_general(score_grad, queries, down, preferred_element_type=jnp.float32)
    dv[span, :] += lax.dot_general(
        attention.astype(jnp.bfloat16), cotangent, down, preferred_element_type=jnp.float32
    )


def chain_kernel(
    n, m, n_rep, rows, longest,
    x_ref, og_ref, qw_ref, kw_ref, vw_ref, dr_ref, dc_ref,
    cols_ref, dqa_ref, kva_ref, ig_ref,
    rs_in, rs_out, og_own, dk, dv, terms, took, done,
    a_send, a_recv, b_send, b_recv, og_send, og_recv, rs_send, rs_recv,
    dq_send, dq_recv, kv_send, kv_recv, r_send, r_recv, e_send, e_recv,
):
    z, c = place(n_rep)
    tok, feats = x_ref.shape
    total = tok * n
    count = total // rows
    per = tok // rows
    piece = rows // m
    q_side = qw_ref.shape[1] // 2
    heads = q_side // DH
    delay = longest // rows
    lead = 2
    half = z // (n // 2)
    e = z * (1 - half) + (n - 1 - z) * half
    f = n - 1 - e
    inner = z + 1 - 2 * half
    outer = z - 1 + 2 * half
    side_b = half
    side_a = 1 - half
    near_end = (n - 1) * half
    far_end = (n - 1) * (1 - half)
    is_end = e == 0
    not_end = e > 0
    f32, bf16 = jnp.float32, jnp.bfloat16

    def chunk_rows(j):
        return rows_at(j * rows, rows)

    def input_copy(u, dq):
        q = (c + dq) % m
        src = x_ref.at[rows_at(u * rows + q * piece, piece)]
        dst = cols_ref.at[rows_at(z * tok + u * rows + q * piece, piece)]
        return src, dst, remote(
            src, dst, a_send.at[u, dq], a_recv.at[z * per + u], device_at(c, q, n_rep)
        )

    def spread_copy(j, d):
        block = cols_ref.at[rows_at(j * rows + c * piece, piece)]
        return remote(
            block, block, b_send.at[j, d], b_recv.at[j, d], device_at(z, (c + d) % m, n_rep)
        )

    def og_copy(u, s, slot, to):
        src = og_ref.at[rows_at(u * rows, rows), cols_at(s * q_side, q_side)]
        dst = og_own.at[chunk_rows(z * per + u)]
        return src, dst, remote(
            src, dst, og_send.at[u, slot], og_recv.at[z * per + u], device_at(to, c, n_rep)
        )

    def rs_copy(s, j, to):
        return remote(
            rs_out.at[s, chunk_rows(j)], rs_in.at[s, chunk_rows(j)],
            rs_send.at[s, j], rs_recv.at[s, j], device_at(to, c, n_rep),
        )

    def dq_copy(s, j, to):
        block = dqa_ref.at[chunk_rows(j), cols_at(s * q_side, q_side)]
        return remote(block, block, dq_send.at[s, j], dq_recv.at[s, j], device_at(to, c, n_rep))

    def kv_copy(s, j, to):
        block = kva_ref.at[:, chunk_rows(j), cols_at(s * DH, DH)]
        return remote(block, block, kv_send.at[s, j], kv_recv.at[s, j], device_at(to, c, n_rep))

    def term_copy(j, d):
        to = (c + d) % m
        return remote(
            terms.at[rows_at(j * rows + to * piece, piece)],
            took.at[d - 1, rows_at(j * piece, piece)],
            r_send.at[j, d], r_recv.at[j, d], device_at(z, to, n_rep),
        )

    def done_place(j):
        return ig_ref.at[rows_at((j % per) * rows + c * piece, piece)]

    def done_copy(j):
        return remote(
            done.at[rows_at(j * piece, piece)], done_place(j),
            e_send.at[j], e_recv.at[c, j % per], device_at(j // per, z, n_rep),
        )

    def spread(j):
        block = cols_ref.at[rows_at(j * rows + c * piece, piece)]
        pltpu.make_async_copy(block, block, a_recv.at[j]).wait()
        for d in range(1, m):
            spread_copy(j, d).start()

    def project(s, j):
        x = cols_ref[chunk_rows(j), :]
        return jnp.concatenate(
            [
                jnp.dot(x, qw_ref[:, cols_at(s * q_side, q_side)], preferred_element_type=f32),
                jnp.dot(x, kw_ref[:, cols_at(s * DH, DH)], preferred_element_type=f32),
                jnp.dot(x, vw_ref[:, cols_at(s * DH, DH)], preferred_element_type=f32),
            ],
            axis=1,
        )

    def reduce_a(j):
        for d in range(1, m):
            spread_copy(j, d).wait_recv()
        part = project(side_a, j)

        @pl.when(is_end)
        def _():
            rs_out[side_a, chunk_rows(j), :] = part.astype(bf16)

        @pl.when(not_end)
        def _():
            rs_copy(side_a, j, inner).wait_recv()
            rs_out[side_a, chunk_rows(j), :] = (
                part + rs_in[side_a, chunk_rows(j), :].astype(f32)
            ).astype(bf16)

        rs_copy(side_a, j, inner).start()

    def reduce_b(j):
        part = project(side_b, j)
        rs_copy(side_b, j, inner).wait_recv()
        rs_out[side_b, chunk_rows(j), :] = (
            part + rs_in[side_b, chunk_rows(j), :].astype(f32)
        ).astype(bf16)

        @pl.when(not_end)
        def _():
            rs_copy(side_b, j, outer).start()

    def settle(i):
        kva_ref[0, chunk_rows(i), cols_at(side_b * DH, DH)] = dk[chunk_rows(i), :].astype(bf16)
        kva_ref[1, chunk_rows(i), cols_at(side_b * DH, DH)] = dv[chunk_rows(i), :].astype(bf16)
        kv_copy(side_b, i, inner).start()

    def attend_chunk(j):
        block = og_own.at[chunk_rows(j)]
        pltpu.make_async_copy(block, block, og_recv.at[j]).wait()
        run = functools.partial(
            attend_rows, heads, rs_out.at[side_b], og_own, dr_ref, dc_ref, dqa_ref, side_b * q_side, dk, dv
        )
        for b in range(delay):
            @pl.when(j == b)
            def _():
                run(b * rows, rows, 0, (b + 1) * rows)

        @pl.when(j >= delay)
        def _():
            run(j * rows, rows, (j - delay) * rows, (delay + 1) * rows)

        dq_copy(side_b, j, inner).start()

        @pl.when(j >= delay)
        def _():
            settle(j - delay)

        @pl.when(j == count - 1)
        def _():
            def rest(i, carry):
                settle(i)
                return carry

            lax.fori_loop(count - delay, count, rest, 0)

    def finish(j):
        for d in range(1, m):
            term_copy(j, d).wait_recv()
        value = terms[rows_at(j * rows + c * piece, piece), :].astype(f32)
        for d in range(1, m):
            value = value + took[d - 1, rows_at(j * piece, piece), :].astype(f32)
        done[rows_at(j * piece, piece), :] = value.astype(bf16)
        own = (j // per == z) & (c == z)

        @pl.when(own)
        def _():
            pltpu.make_async_copy(
                done.at[rows_at(j * piece, piece)], done_place(j), e_recv.at[c, j % per]
            ).start()

        @pl.when(jnp.logical_not(own))
        def _():
            done_copy(j).start()

    def term(j):
        across = (((1,), (1,)), ((), ()))
        value = lax.dot_general(
            dqa_ref[chunk_rows(j), :], qw_ref[...], across, preferred_element_type=f32
        )
        value = value + lax.dot_general(
            kva_ref[0, chunk_rows(j), :], kw_ref[...], across, preferred_element_type=f32
        )
        value = value + lax.dot_general(
            kva_ref[1, chunk_rows(j), :], vw_ref[...], across, preferred_element_type=f32
        )
        terms[chunk_rows(j), :] = value.astype(bf16)
        for d in range(1, m):
            term_copy(j, d).start()

        @pl.when(j > 0)
        def _():
            finish(j - 1)

    def pass_pair_b(i):
        kv_copy(side_b, i, inner).wait_recv()
        kv_copy(side_b, i, inner).start()

    def pass_pair_a(i):
        kv_copy(side_a, i, inner).wait_recv()

        @pl.when(not_end)
        def _():
            kv_copy(side_a, i, outer).start()

        term(i)

    greet(n, m, n_rep)
    own = c == z
    for u in range(per):
        for dq in range(m):
            src, dst, copy = input_copy(u, dq)
            if dq == 0:
                @pl.when(own)
                def _():
                    pltpu.make_async_copy(src, dst, a_recv.at[z * per + u]).start()

                @pl.when(jnp.logical_not(own))
                def _():
                    copy.start()
            else:
                copy.start()

    @pl.when(is_end)
    def _():
        dk[...] = jnp.zeros_like(dk)
        dv[...] = jnp.zeros_like(dv)

    for j in range(lead):
        spread(j)

    def step(k, carry):
        u = k - z * per

        @pl.when((k >= z * per) & (k < z * per + per))
        def _():
            _, _, copy = og_copy(u, side_a, 0, far_end)
            copy.start()
            src, dst, copy = og_copy(u, side_b, 1, near_end)

            @pl.when(is_end)
            def _():
                pltpu.make_async_copy(src, dst, og_recv.at[z * per + u]).start()

            @pl.when(not_end)
            def _():
                copy.start()

        @pl.when((k >= e) & (k < e + count))
        def _():
            reduce_a(k - e)

        @pl.when(k + lead < count)
        def _():
            spread(k + lead)

        @pl.when((k >= f) & (k < f + count))
        def _():
            reduce_b(k - f)

        @pl.when(is_end & (k >= n - 1) & (k < n - 1 + count))
        def _():
            attend_chunk(k - (n - 1))

        jb = k - (n - 1) - e

        @pl.when(not_end & (k >= n - 1 + e) & (k < n - 1 + e + count))
        def _():
            dq_copy(side_b, jb, inner).wait_recv()
            dq_copy(side_b, jb, inner).start()

            @pl.when(jb >= delay)
            def _():
                pass_pair_b(jb - delay)

            @pl.when(jb == count - 1)
            def _():
                def rest(i, carry):
                    pass_pair_b(i)
                    return carry

                lax.fori_loop(count - delay, count, rest, 0)

        ja = k - (n - 1) - f

        @pl.when((k >= n - 1 + f) & (k < n - 1 + f + count))
        def _():
            dq_copy(side_a, ja, inner).wait_recv()

            @pl.when(not_end)
            def _():
                dq_copy(side_a, ja, outer).start()

            @pl.when(ja >= delay)
            def _():
                first = ja - delay
                last = first + 1 + delay * (ja // (count - 1))

                def rest(i, carry):
                    pass_pair_a(i)
                    return carry

                lax.fori_loop(first, last, rest, 0)

        return carry

    lax.fori_loop(0, count + 2 * (n - 1), step, 0)
    finish(jnp.int32(count - 1))

    def drain(j, carry):
        for d in range(1, m):
            spread_copy(j, d).wait_send()
            term_copy(j, d).wait_send()
        rs_copy(side_a, j, inner).wait_send()
        dq_copy(side_b, j, inner).wait_send()
        kv_copy(side_b, j, inner).wait_send()

        @pl.when(not_end)
        def _():
            rs_copy(side_b, j, outer).wait_send()
            dq_copy(side_a, j, outer).wait_send()
            kv_copy(side_a, j, outer).wait_send()

        @pl.when(jnp.logical_not((j // per == z) & (c == z)))
        def _():
            done_copy(j).wait_send()

        return carry

    lax.fori_loop(0, count, drain, 0)
    for u in range(per):
        _, _, copy = og_copy(u, side_a, 0, far_end)
        copy.wait_send()

        @pl.when(not_end)
        def _():
            _, _, copy = og_copy(u, side_b, 1, near_end)
            copy.wait_send()

        for dq in range(m):
            _, _, copy = input_copy(u, dq)
            if dq == 0:
                @pl.when(jnp.logical_not(own))
                def _():
                    copy.wait_send()
            else:
                copy.wait_send()
        for q in range(m):
            block = ig_ref.at[u * rows + q * piece : u * rows + (q + 1) * piece]
            pltpu.make_async_copy(block, block, e_recv.at[q, u]).wait()


def chained(n, n_hid, n_rep, layer_input, query_weight, key_weight, value_weight, out_grad, doc_ids):
    m = n_hid * n_rep
    bf16, f32 = jnp.bfloat16, jnp.float32
    tok, feats = layer_input.shape
    total = tok * n
    rows = BLOCK
    count, per, piece = total // rows, tok // rows, rows // m
    q_cols = query_weight.shape[1]
    pair_width = key_weight.shape[1]
    width = q_cols // 2 + pair_width
    dma = pltpu.SemaphoreType.DMA
    columns, queries_all, pairs_all, input_grad = pl.pallas_call(
        functools.partial(chain_kernel, n, m, n_rep, rows, total // 2),
        out_shape=(
            jax.ShapeDtypeStruct((total, feats), bf16),
            jax.ShapeDtypeStruct((total, q_cols), bf16),
            jax.ShapeDtypeStruct((2, total, pair_width), bf16),
            jax.ShapeDtypeStruct((tok, feats), bf16),
        ),
        in_specs=[VM] * 7,
        out_specs=(VM,) * 4,
        scratch_shapes=[
            pltpu.VMEM((2, total, width), bf16),
            pltpu.VMEM((2, total, width), bf16),
            pltpu.VMEM((total, q_cols // 2), bf16),
            pltpu.VMEM((total, DH), f32),
            pltpu.VMEM((total, DH), f32),
            pltpu.VMEM((total, feats), bf16),
            pltpu.VMEM((m - 1, count * piece, feats), bf16),
            pltpu.VMEM((count * piece, feats), bf16),
            dma((per, m)), dma((count,)), dma((count, m)), dma((count, m)),
            dma((per, 2)), dma((count,)), dma((2, count)), dma((2, count)),
            dma((2, count)), dma((2, count)), dma((2, count)), dma((2, count)),
            dma((count, m)), dma((count, m)), dma((count,)), dma((m, per)),
        ],
        compiler_params=pltpu.CompilerParams(
            collective_id=0, has_side_effects=True, vmem_limit_bytes=VMEM_BYTES
        ),
    )(
        layer_input, out_grad, query_weight, key_weight, value_weight,
        doc_ids.reshape(total, 1), doc_ids.reshape(1, total),
    )

    def weight_grad(grads):
        return lax.dot_general(
            columns, grads, (((0,), (0,)), ((), ())), preferred_element_type=f32
        )

    return (
        input_grad,
        weight_grad(queries_all),
        weight_grad(pairs_all[0]),
        weight_grad(pairs_all[1]),
    )


def solution(mesh):
    in_specs = (
        P(("groups", "srv"), ("hid", "rep")),
        P("srv", ("hid", "rep")),
        P("srv", ("hid", "rep")),
        P("srv", ("hid", "rep")),
        P(("groups", "srv"), ("hid", "rep")),
        P("groups"),
    )
    out_specs = (
        P(("groups", "srv"), ("hid", "rep")),
        P(("groups", "srv"), ("hid", "rep")),
        P(("groups", "srv"), ("hid", "rep")),
        P(("groups", "srv"), ("hid", "rep")),
    )
    n, n_hid, n_rep = mesh.shape["srv"], mesh.shape["hid"], mesh.shape["rep"]
    m = n_hid * n_rep
    inner = body
    if n == m and n > 2 and n % 2 == 0 and HK == 2 * m and HQ % HK == 0:
        inner = functools.partial(chained, n, n_hid, n_rep)
    return jax.shard_map(inner, mesh=mesh, in_specs=in_specs, out_specs=out_specs, check_vma=False)
```

time: 203 us -> 164 us (0.81)
  Pallas kernels: 190 us -> 151 us
    pallas_call x3 -> x1, Pallas kernels: 190 us -> 151 us  [chained(): pl.pallas_call(functools.partial(chain_kernel, n, m, n_rep, rows, total /...]
where the time goes in v1:
time: 164 us
  Pallas kernels  151 us (92%)
  matrix products  10.2 us (6%)
  local copies, waits for them, and re-layouts  2.51 us (2%)
    pallas_call x1, Pallas kernels, chained(): pl.pallas_call(functools.partial(chain_kernel, n, m, n_rep, rows, total /...  151 us
    dot_general x3, matrix products, weight_grad(): lax.dot_general(columns, grads, (((0,), (0,)), ((), ())), preferred_eleme...  10.2 us

profile of v1, /device:TPU:0, one launch (start us, length us, event | category | flops | bytes accessed | tf_op | source)
XLA Modules:
  0.0 164.2 jit_solution(12832262791461067)
XLA Ops:
  0.6 1.7 %copy.10.dr_ref = s32[1024,1]{1,0:T(8,128)} copy(s32[1024,1]{0,1:T(1,128)} %bitcast.12) | data formatting | bytes 8192 | tf_op jit(solution)/shard_map/reshape | solution.py:664
  2.3 150.8 %shard_map.93 = (bf16[1024,1024]{1,0:T(8,128)(2,1)}, bf16[1024,1024]{1,0:T(8,128)(2,1)}, bf16[2,1024,256]{2,1,0:T(8,128)(2,1)}, bf16[256,1024]{1,0:T(8,128)(2,1)}) custom-call(bf16[256,1024]{1,0:T(8,128)(2,1)} %x_ref.1, bf16[256,1024]{1,0:T(8,128)(2,1)} %og_ref.1, bf16[1024,1024]{1,0:T(8,128)(2,1)} %qw_ref.1, bf16[1024,256]{1,0:T(8,128)(2,1)} %kw_ref.1, ...), custom_call_target="tpu_custom_call" | custom-call | tf_op jit(solution)/shard_map/pallas_call | solution.py:635
  153.1 0.0 copy-start.1
  153.1 0.0 copy-start.2
  153.2 6.8 %fusion.6 = f32[1024,1024]{1,0:T(8,128)} fusion(bf16[1024,1024]{1,0:T(8,128)(2,1)} %get-tuple-element.9, bf16[1024,1024]{1,0:T(8,128)(2,1)} %get-tuple-element.10), kind=kOutput, calls=%fused_computation.6 | convolution fusion | flops 2147483648 | bytes 8388608 | tf_op jit(solution)/shard_map/dot_general | solution.py:668
  159.9 0.0 copy-done.1
  159.9 0.0 copy-done.2
  159.9 1.7 %fusion.2 = f32[1024,256]{1,0:T(8,128)} fusion(bf16[1024,1024]{1,0:T(8,128)(2,1)S(1)} %copy-done.1, bf16[2,1024,256]{2,1,0:T(8,128)(2,1)S(1)} %copy-done.2), kind=kOutput, calls=%fused_computation.2 | convolution fusion | flops 536870912 | bytes 3670016 | tf_op jit(solution)/shard_map/dot_general | solution.py:668
  161.6 0.0 copy-start
  161.6 1.7 %fusion = f32[1024,256]{1,0:T(8,128)} fusion(bf16[1024,1024]{1,0:T(8,128)(2,1)S(1)} %copy-done.1, bf16[2,1024,256]{2,1,0:T(8,128)(2,1)S(1)} %copy-done.2), kind=kOutput, calls=%fused_computation | convolution fusion | flops 536870912 | bytes 3670016 | tf_op jit(solution)/shard_map/dot_general | solution.py:668
  163.4 0.0 copy-done
  163.4 0.8 copy.12
Async XLA Ops:
  153.1 6.8 %copy-start.1 = (bf16[1024,1024]{1,0:T(8,128)(2,1)S(1)}, bf16[1024,1024]{1,0:T(8,128)(2,1)}, u32[]{:S(2)}) copy-start(bf16[1024,1024]{1,0:T(8,128)(2,1)} %get-tuple-element.9) | copy-start | bytes 6291460
  153.1 6.8 %copy-start.2 = (bf16[2,1024,256]{2,1,0:T(8,128)(2,1)S(1)}, bf16[2,1024,256]{2,1,0:T(8,128)(2,1)}, u32[]{:S(2)}) copy-start(bf16[2,1024,256]{2,1,0:T(8,128)(2,1)} %get-tuple-element.11) | copy-start | bytes 3145732
  161.6 1.7 %copy-start = (bf16[256,1024]{1,0:T(8,128)(2,1)S(1)}, bf16[256,1024]{1,0:T(8,128)(2,1)}, u32[]{:S(2)}) copy-start(bf16[256,1024]{1,0:T(8,128)(2,1)} %get-tuple-element.16) | copy-start | bytes 1572868

commit v2 on v1

--- a/solution.py
+++ b/solution.py
@@ -229,7 +229,7 @@
     return pl.ds(pl.multiple_of(start, DH), size)
 
 
-def attend_rows(heads, qkv, og_ref, dr_ref, dc_ref, dq_ref, dq_cols, dk, dv, first, row_block, low, width):
+def attend_rows(heads, qkv, og_ref, dc_ref, dq_ref, dq_cols, dk, dv, first, row_block, low, width):
     q_cols = heads * DH
     scale = DH ** (-0.5)
     rows = rows_at(first, row_block)
@@ -240,7 +240,8 @@
     values = qkv[span, q_cols + DH : q_cols + 2 * DH]
     row_pos = first + lax.broadcasted_iota(jnp.int32, (row_block, width), 0)
     key_pos = low + lax.broadcasted_iota(jnp.int32, (row_block, width), 1)
-    kept = (dr_ref[rows, :] == dc_ref[:, span]) & (key_pos <= row_pos)
+    row_doc = jnp.broadcast_to(dc_ref[:, rows].astype(jnp.float32), (row_block, row_block)).T[:, :1]
+    kept = (row_doc == dc_ref[:, span].astype(jnp.float32)) & (key_pos <= row_pos)
     bias = jnp.concatenate([jnp.where(kept, 0.0, NEGATIVE)] * heads, axis=0)
     both = (((1,), (1,)), ((), ()))
     logits = lax.dot_general(queries, keys, both, preferred_element_type=jnp.float32) * scale + bias
@@ -261,11 +262,11 @@
 
 def chain_kernel(
     n, m, n_rep, rows, longest,
-    x_ref, og_ref, qw_ref, kw_ref, vw_ref, dr_ref, dc_ref,
-    cols_ref, dqa_ref, kva_ref, ig_ref,
-    rs_in, rs_out, og_own, dk, dv, terms, took, done,
-    a_send, a_recv, b_send, b_recv, og_send, og_recv, rs_send, rs_recv,
-    dq_send, dq_recv, kv_send, kv_recv, r_send, r_recv, e_send, e_recv,
+    x_ref, og_ref, qw_in, kw_in, vw_in, dc_ref,
+    turned_out, dqa_out, kva_out, ig_ref,
+    qw_ref, kw_ref, vw_ref, cols_ref, turned, dqa_ref, kva_ref, rs_in, rs_out, og_own, dk, dv, hopped, terms, took, paired, done,
+    h_send, h_recv, a_send, a_recv, b_send, b_recv, og_send, og_recv, rs_send, rs_recv,
+    dq_send, dq_recv, kv_send, kv_recv, r_send, r_recv, e_send, e_recv, out_sem, w_sem,
 ):
     z, c = place(n_rep)
     tok, feats = x_ref.shape
@@ -273,10 +274,12 @@
     count = total // rows
     per = tok // rows
     piece = rows // m
+    parts = tok // (rows // 2)
+    share = piece // 2
     q_side = qw_ref.shape[1] // 2
     heads = q_side // DH
     delay = longest // rows
-    lead = 2
+    lead = 5
     half = z // (n // 2)
     e = z * (1 - half) + (n - 1 - z) * half
     f = n - 1 - e
@@ -288,23 +291,48 @@
     far_end = (n - 1) * (1 - half)
     is_end = e == 0
     not_end = e > 0
+    sibling = c + 1 - 2 * (c % 2)
+    across = (c + 2) % m
+    diagonal = across + 1 - 2 * (across % 2)
+    sub = rows // 2
     f32, bf16 = jnp.float32, jnp.bfloat16
 
     def chunk_rows(j):
         return rows_at(j * rows, rows)
 
-    def input_copy(u, dq):
-        q = (c + dq) % m
-        src = x_ref.at[rows_at(u * rows + q * piece, piece)]
-        dst = cols_ref.at[rows_at(z * tok + u * rows + q * piece, piece)]
-        return src, dst, remote(
-            src, dst, a_send.at[u, dq], a_recv.at[z * per + u], device_at(c, q, n_rep)
-        )
-
-    def spread_copy(j, d):
-        block = cols_ref.at[rows_at(j * rows + c * piece, piece)]
+    def hop_copy(u):
+        src = x_ref.at[rows_at(u * sub + (across // 2) * 2 * share, 2 * share)]
+        return remote(src, hopped.at[u], h_send.at[u], h_recv.at[u], device_at(z, across, n_rep))
+
+    def input_copy(u, i, direct):
+        p = (c // 2) * 2 + i
+        plane = c if direct else across
+        if direct:
+            src = x_ref.at[rows_at(u * sub + p * share, share)]
+        else:
+            src = hopped.at[u, i * share : (i + 1) * share]
+        dst = cols_ref.at[rows_at(z * tok + u * sub + p * share, share)]
+        copy = remote(
+            src, dst, a_send.at[u, i, int(direct)], a_recv.at[z * parts + u], device_at(plane, p, n_rep)
+        )
+        return (plane == z) & (p == c), src, dst, copy
+
+    def send_input(u, i, direct):
+        own, src, dst, copy = input_copy(u, i, direct)
+
+        @pl.when(own)
+        def _():
+            pltpu.make_async_copy(src, dst, a_recv.at[z * parts + u]).start()
+
+        @pl.when(jnp.logical_not(own))
+        def _():
+            copy.start()
+
+    def spread_copy(g, slot):
+        owner, to = ((c, sibling), (c, across), (across, sibling))[slot]
+        block = cols_ref.at[rows_at(g * sub + owner * share, share)]
         return remote(
-            block, block, b_send.at[j, d], b_recv.at[j, d], device_at(z, (c + d) % m, n_rep)
+            block, block, b_send.at[g, slot], b_recv.at[g, slot], device_at(z, to, n_rep)
         )
 
     def og_copy(u, s, slot, to):
@@ -314,10 +342,13 @@
             src, dst, og_send.at[u, slot], og_recv.at[z * per + u], device_at(to, c, n_rep)
         )
 
-    def rs_copy(s, j, to):
+    def sub_rows(g):
+        return rows_at(g * sub, sub)
+
+    def rs_copy(s, g, to):
         return remote(
-            rs_out.at[s, chunk_rows(j)], rs_in.at[s, chunk_rows(j)],
-            rs_send.at[s, j], rs_recv.at[s, j], device_at(to, c, n_rep),
+            rs_out.at[s, sub_rows(g)], rs_in.at[s, sub_rows(g)],
+            rs_send.at[s, g], rs_recv.at[s, g], device_at(to, c, n_rep),
         )
 
     def dq_copy(s, j, to):
@@ -328,12 +359,21 @@
         block = kva_ref.at[:, chunk_rows(j), cols_at(s * DH, DH)]
         return remote(block, block, kv_send.at[s, j], kv_recv.at[s, j], device_at(to, c, n_rep))
 
-    def term_copy(j, d):
-        to = (c + d) % m
+    def term_rows(j, owner):
+        return rows_at(j * rows + owner * piece, piece)
+
+    def term_copy(j, slot):
         return remote(
-            terms.at[rows_at(j * rows + to * piece, piece)],
-            took.at[d - 1, rows_at(j * piece, piece)],
-            r_send.at[j, d], r_recv.at[j, d], device_at(z, to, n_rep),
+            terms.at[term_rows(j, diagonal if slot else sibling)],
+            took.at[slot, rows_at(j * piece, piece)],
+            r_send.at[j, slot], r_recv.at[j, slot], device_at(z, sibling, n_rep),
+        )
+
+    def pair_copy(j):
+        block = rows_at(j * piece, piece)
+        return remote(
+            paired.at[block], took.at[2, block],
+            r_send.at[j, 2], r_recv.at[j, 2], device_at(z, across, n_rep),
         )
 
     def done_place(j):
@@ -345,14 +385,18 @@
             e_send.at[j], e_recv.at[c, j % per], device_at(j // per, z, n_rep),
         )
 
-    def spread(j):
-        block = cols_ref.at[rows_at(j * rows + c * piece, piece)]
-        pltpu.make_async_copy(block, block, a_recv.at[j]).wait()
-        for d in range(1, m):
-            spread_copy(j, d).start()
-
-    def project(s, j):
-        x = cols_ref[chunk_rows(j), :]
+    def spread(g):
+        block = cols_ref.at[rows_at(g * sub + c * share, share)]
+        pltpu.make_async_copy(block, block, a_recv.at[g]).wait()
+        for slot in (1, 0):
+            spread_copy(g, slot).start()
+
+    def relay(j):
+        spread_copy(j, 1).wait_recv()
+        spread_copy(j, 2).start()
+
+    def project(s, g):
+        x = cols_ref[sub_rows(g), :]
         return jnp.concatenate(
             [
                 jnp.dot(x, qw_ref[:, cols_at(s * q_side, q_side)], preferred_element_type=f32),
@@ -362,34 +406,40 @@
             axis=1,
         )
 
-    def reduce_a(j):
-        for d in range(1, m):
-            spread_copy(j, d).wait_recv()
-        part = project(side_a, j)
+    def add_in(s, g):
+        part = project(s, g)
+        rs_copy(s, g, inner).wait_recv()
+        rs_out[s, sub_rows(g), :] = (part + rs_in[s, sub_rows(g), :].astype(f32)).astype(bf16)
+
+    def out_copy(j, slot):
+        if slot == 2:
+            src, dst = kva_ref.at[:, chunk_rows(j)], kva_out.at[:, chunk_rows(j)]
+        elif slot == 1:
+            src, dst = dqa_ref.at[chunk_rows(j)], dqa_out.at[chunk_rows(j)]
+        else:
+            src, dst = turned.at[:, chunk_rows(j)], turned_out.at[:, chunk_rows(j)]
+        return pltpu.make_async_copy(src, dst, out_sem.at[j, slot])
+
+    def reduce_a(g):
+        for slot in (0, 2):
+            spread_copy(g, slot).wait_recv()
 
         @pl.when(is_end)
         def _():
-            rs_out[side_a, chunk_rows(j), :] = part.astype(bf16)
+            rs_out[side_a, sub_rows(g), :] = project(side_a, g).astype(bf16)
 
         @pl.when(not_end)
         def _():
-            rs_copy(side_a, j, inner).wait_recv()
-            rs_out[side_a, chunk_rows(j), :] = (
-                part + rs_in[side_a, chunk_rows(j), :].astype(f32)
-            ).astype(bf16)
-
-        rs_copy(side_a, j, inner).start()
-
-    def reduce_b(j):
-        part = project(side_b, j)
-        rs_copy(side_b, j, inner).wait_recv()
-        rs_out[side_b, chunk_rows(j), :] = (
-            part + rs_in[side_b, chunk_rows(j), :].astype(f32)
-        ).astype(bf16)
+            add_in(side_a, g)
+
+        rs_copy(side_a, g, inner).start()
+
+    def reduce_b(g):
+        add_in(side_b, g)
 
         @pl.when(not_end)
         def _():
-            rs_copy(side_b, j, outer).start()
+            rs_copy(side_b, g, outer).start()
 
     def settle(i):
         kva_ref[0, chunk_rows(i), cols_at(side_b * DH, DH)] = dk[chunk_rows(i), :].astype(bf16)
@@ -400,7 +450,7 @@
         block = og_own.at[chunk_rows(j)]
         pltpu.make_async_copy(block, block, og_recv.at[j]).wait()
         run = functools.partial(
-            attend_rows, heads, rs_out.at[side_b], og_own, dr_ref, dc_ref, dqa_ref, side_b * q_side, dk, dv
+            attend_rows, heads, rs_out.at[side_b], og_own, dc_ref, dqa_ref, side_b * q_side, dk, dv
         )
         for b in range(delay):
             @pl.when(j == b)
@@ -425,12 +475,19 @@
 
             lax.fori_loop(count - delay, count, rest, 0)
 
+    def combine(j):
+        term_copy(j, 1).wait_recv()
+        block = rows_at(j * piece, piece)
+        value = terms[term_rows(j, across), :].astype(f32) + took[1, block, :].astype(f32)
+        paired[block, :] = value.astype(bf16)
+        pair_copy(j).start()
+
     def finish(j):
-        for d in range(1, m):
-            term_copy(j, d).wait_recv()
-        value = terms[rows_at(j * rows + c * piece, piece), :].astype(f32)
-        for d in range(1, m):
-            value = value + took[d - 1, rows_at(j * piece, piece), :].astype(f32)
+        block = rows_at(j * piece, piece)
+        term_copy(j, 0).wait_recv()
+        value = terms[term_rows(j, c), :].astype(f32) + took[0, block, :].astype(f32)
+        pair_copy(j).wait_recv()
+        value = value + took[2, block, :].astype(f32)
         done[rows_at(j * piece, piece), :] = value.astype(bf16)
         own = (j // per == z) & (c == z)
 
@@ -445,70 +502,90 @@
             done_copy(j).start()
 
     def term(j):
-        across = (((1,), (1,)), ((), ()))
+        for slot in (1, 2):
+            out_copy(j, slot).start()
+        flip = (((1,), (1,)), ((), ()))
         value = lax.dot_general(
-            dqa_ref[chunk_rows(j), :], qw_ref[...], across, preferred_element_type=f32
+            dqa_ref[chunk_rows(j), :], qw_ref[...], flip, preferred_element_type=f32
         )
         value = value + lax.dot_general(
-            kva_ref[0, chunk_rows(j), :], kw_ref[...], across, preferred_element_type=f32
+            kva_ref[0, chunk_rows(j), :], kw_ref[...], flip, preferred_element_type=f32
         )
         value = value + lax.dot_general(
-            kva_ref[1, chunk_rows(j), :], vw_ref[...], across, preferred_element_type=f32
+            kva_ref[1, chunk_rows(j), :], vw_ref[...], flip, preferred_element_type=f32
         )
         terms[chunk_rows(j), :] = value.astype(bf16)
-        for d in range(1, m):
-            term_copy(j, d).start()
+        for slot in (1, 0):
+            term_copy(j, slot).start()
 
         @pl.when(j > 0)
         def _():
-            finish(j - 1)
-
-    def pass_pair_b(i):
-        kv_copy(side_b, i, inner).wait_recv()
-        kv_copy(side_b, i, inner).start()
-
-    def pass_pair_a(i):
-        kv_copy(side_a, i, inner).wait_recv()
-
-        @pl.when(not_end)
-        def _():
-            kv_copy(side_a, i, outer).start()
-
-        term(i)
-
+            combine(j - 1)
+
+        @pl.when(j > 1)
+        def _():
+            finish(j - 2)
+
+    def pass_b(v):
+        @pl.when(v < count)
+        def _():
+            dq_copy(side_b, v, inner).wait_recv()
+            dq_copy(side_b, v, inner).start()
+
+        @pl.when(v >= delay)
+        def _():
+            kv_copy(side_b, v - delay, inner).wait_recv()
+            kv_copy(side_b, v - delay, inner).start()
+
+    def pass_a(v):
+        @pl.when(v < count)
+        def _():
+            dq_copy(side_a, v, inner).wait_recv()
+
+            @pl.when(not_end)
+            def _():
+                dq_copy(side_a, v, outer).start()
+
+        @pl.when(v >= delay)
+        def _():
+            kv_copy(side_a, v - delay, inner).wait_recv()
+
+            @pl.when(not_end)
+            def _():
+                kv_copy(side_a, v - delay, outer).start()
+
+            term(v - delay)
+
+    loads = [
+        pltpu.make_async_copy(qw_in, qw_ref, w_sem.at[0]),
+        pltpu.make_async_copy(kw_in, kw_ref, w_sem.at[1]),
+        pltpu.make_async_copy(vw_in, vw_ref, w_sem.at[2]),
+    ]
+    for copy in loads:
+        copy.start()
     greet(n, m, n_rep)
-    own = c == z
-    for u in range(per):
-        for dq in range(m):
-            src, dst, copy = input_copy(u, dq)
-            if dq == 0:
-                @pl.when(own)
-                def _():
-                    pltpu.make_async_copy(src, dst, a_recv.at[z * per + u]).start()
-
-                @pl.when(jnp.logical_not(own))
-                def _():
-                    copy.start()
-            else:
-                copy.start()
+    for u in range(parts):
+        hop_copy(u).start()
+    for u in range(parts):
+        for i in range(2):
+            send_input(u, i, True)
 
     @pl.when(is_end)
     def _():
         dk[...] = jnp.zeros_like(dk)
         dv[...] = jnp.zeros_like(dv)
 
-    for j in range(lead):
-        spread(j)
-
-    def step(k, carry):
-        u = k - z * per
-
-        @pl.when((k >= z * per) & (k < z * per + per))
-        def _():
-            _, _, copy = og_copy(u, side_a, 0, far_end)
+    def forward(u):
+        hop_copy(u).wait_recv()
+        for i in range(2):
+            send_input(u, i, False)
+
+    def send_og(u, slot):
+        to = (far_end, near_end)[slot]
+        src, dst, copy = og_copy(u, (side_a, side_b)[slot], slot, to)
+        if slot == 0:
             copy.start()
-            src, dst, copy = og_copy(u, side_b, 1, near_end)
-
+        else:
             @pl.when(is_end)
             def _():
                 pltpu.make_async_copy(src, dst, og_recv.at[z * per + u]).start()
@@ -517,78 +594,92 @@
             def _():
                 copy.start()
 
-        @pl.when((k >= e) & (k < e + count))
-        def _():
-            reduce_a(k - e)
-
-        @pl.when(k + lead < count)
+    forward(0)
+    forward(1)
+    spread(0)
+    for u in range(2, parts):
+        forward(u)
+    for g in range(1, lead):
+        spread(g)
+    for g in range(2):
+        relay(g)
+    for u in range(per):
+        send_og(u, 1)
+
+        @pl.when(not_end)
+        def _():
+            send_og(u, 0)
+    for copy in loads:
+        copy.wait()
+
+    def step(k, carry):
+        even = k % 2 == 0
+        j = k // 2
+
+        @pl.when(is_end & even & (j > 0) & (j <= per))
+        def _():
+            send_og(j - 1, 0)
+
+        @pl.when(k + 2 < 2 * count)
+        def _():
+            relay(k + 2)
+
+        @pl.when((k >= 2 * e) & (k < 2 * e + 2 * count))
+        def _():
+            reduce_a(k - 2 * e)
+
+        @pl.when(k + lead < 2 * count)
         def _():
             spread(k + lead)
 
-        @pl.when((k >= f) & (k < f + count))
-        def _():
-            reduce_b(k - f)
-
-        @pl.when(is_end & (k >= n - 1) & (k < n - 1 + count))
-        def _():
-            attend_chunk(k - (n - 1))
-
-        jb = k - (n - 1) - e
-
-        @pl.when(not_end & (k >= n - 1 + e) & (k < n - 1 + e + count))
-        def _():
-            dq_copy(side_b, jb, inner).wait_recv()
-            dq_copy(side_b, jb, inner).start()
-
-            @pl.when(jb >= delay)
-            def _():
-                pass_pair_b(jb - delay)
-
-            @pl.when(jb == count - 1)
-            def _():
-                def rest(i, carry):
-                    pass_pair_b(i)
-                    return carry
-
-                lax.fori_loop(count - delay, count, rest, 0)
-
-        ja = k - (n - 1) - f
-
-        @pl.when((k >= n - 1 + f) & (k < n - 1 + f + count))
-        def _():
-            dq_copy(side_a, ja, inner).wait_recv()
-
-            @pl.when(not_end)
-            def _():
-                dq_copy(side_a, ja, outer).start()
-
-            @pl.when(ja >= delay)
-            def _():
-                first = ja - delay
-                last = first + 1 + delay * (ja // (count - 1))
-
-                def rest(i, carry):
-                    pass_pair_a(i)
-                    return carry
-
-                lax.fori_loop(first, last, rest, 0)
+        @pl.when((k % 2 == 1) & (k >= 2 * e) & (k < 2 * e + 2 * count))
+        def _():
+            turned[:, chunk_rows(j - e)] = cols_ref[chunk_rows(j - e), :].T
+            out_copy(j - e, 0).start()
+
+        @pl.when((k >= 2 * f) & (k < 2 * f + 2 * count))
+        def _():
+            reduce_b(k - 2 * f)
+
+        h = j + 1
+
+        @pl.when(is_end & (k % 2 == 1) & (h >= n) & (h < n + count))
+        def _():
+            attend_chunk(h - n)
+
+        @pl.when(not_end & (k % 2 == 1) & (h >= n + e) & (h < n + e + count + delay))
+        def _():
+            pass_b(h - n - e)
+
+        @pl.when((k % 2 == 1) & (h >= n + f) & (h < n + f + count + delay))
+        def _():
+            pass_a(h - n - f)
 
         return carry
 
-    lax.fori_loop(0, count + 2 * (n - 1), step, 0)
+    lax.fori_loop(0, 2 * (count + delay + 2 * (n - 1) + 1), step, 0)
+    combine(jnp.int32(count - 1))
+    finish(jnp.int32(count - 2))
     finish(jnp.int32(count - 1))
 
     def drain(j, carry):
-        for d in range(1, m):
-            spread_copy(j, d).wait_send()
-            term_copy(j, d).wait_send()
-        rs_copy(side_a, j, inner).wait_send()
+        for slot in range(3):
+            spread_copy(2 * j, slot).wait_send()
+            spread_copy(2 * j + 1, slot).wait_send()
+        for slot in range(2):
+            term_copy(j, slot).wait_send()
+        pair_copy(j).wait_send()
+        for i in range(2):
+            rs_copy(side_a, 2 * j + i, inner).wait_send()
+        for slot in range(3):
+            out_copy(j, slot).wait()
         dq_copy(side_b, j, inner).wait_send()
         kv_copy(side_b, j, inner).wait_send()
 
         @pl.when(not_end)
         def _():
-            rs_copy(side_b, j, outer).wait_send()
+            for i in range(2):
+                rs_copy(side_b, 2 * j + i, outer).wait_send()
             dq_copy(side_a, j, outer).wait_send()
             kv_copy(side_a, j, outer).wait_send()
 
@@ -599,6 +690,15 @@
         return carry
 
     lax.fori_loop(0, count, drain, 0)
+    for u in range(parts):
+        hop_copy(u).wait_send()
+        for i in range(2):
+            for direct in (True, False):
+                own, _, _, copy = input_copy(u, i, direct)
+
+                @pl.when(jnp.logical_not(own))
+                def _():
+                    copy.wait_send()
     for u in range(per):
         _, _, copy = og_copy(u, side_a, 0, far_end)
         copy.wait_send()
@@ -608,14 +708,6 @@
             _, _, copy = og_copy(u, side_b, 1, near_end)
             copy.wait_send()
 
-        for dq in range(m):
-            _, _, copy = input_copy(u, dq)
-            if dq == 0:
-                @pl.when(jnp.logical_not(own))
-                def _():
-                    copy.wait_send()
-            else:
-                copy.wait_send()
         for q in range(m):
             block = ig_ref.at[u * rows + q * piece : u * rows + (q + 1) * piece]
             pltpu.make_async_copy(block, block, e_recv.at[q, u]).wait()
@@ -632,49 +724,81 @@
     pair_width = key_weight.shape[1]
     width = q_cols // 2 + pair_width
     dma = pltpu.SemaphoreType.DMA
-    columns, queries_all, pairs_all, input_grad = pl.pallas_call(
+    ANY = pl.BlockSpec(memory_space=pl.ANY)
+    turned, queries_all, pairs_all, input_grad = pl.pallas_call(
         functools.partial(chain_kernel, n, m, n_rep, rows, total // 2),
         out_shape=(
-            jax.ShapeDtypeStruct((total, feats), bf16),
+            jax.ShapeDtypeStruct((feats, total), bf16),
             jax.ShapeDtypeStruct((total, q_cols), bf16),
             jax.ShapeDtypeStruct((2, total, pair_width), bf16),
             jax.ShapeDtypeStruct((tok, feats), bf16),
         ),
-        in_specs=[VM] * 7,
-        out_specs=(VM,) * 4,
+        in_specs=[ANY] * 5 + [VM],
+        out_specs=(ANY,) * 4,
         scratch_shapes=[
+            pltpu.VMEM(query_weight.shape, bf16),
+            pltpu.VMEM(key_weight.shape, bf16),
+            pltpu.VMEM(value_weight.shape, bf16),
+            pltpu.VMEM((total, feats), bf16),
+            pltpu.VMEM((feats, total), bf16),
+            pltpu.VMEM((total, q_cols), bf16),
+            pltpu.VMEM((2, total, pair_width), bf16),
             pltpu.VMEM((2, total, width), bf16),
             pltpu.VMEM((2, total, width), bf16),
             pltpu.VMEM((total, q_cols // 2), bf16),
             pltpu.VMEM((total, DH), f32),
             pltpu.VMEM((total, DH), f32),
+            pltpu.VMEM((2 * per, rows // 4, feats), bf16),
             pltpu.VMEM((total, feats), bf16),
-            pltpu.VMEM((m - 1, count * piece, feats), bf16),
+            pltpu.VMEM((3, count * piece, feats), bf16),
             pltpu.VMEM((count * piece, feats), bf16),
-            dma((per, m)), dma((count,)), dma((count, m)), dma((count, m)),
-            dma((per, 2)), dma((count,)), dma((2, count)), dma((2, count)),
+            pltpu.VMEM((count * piece, feats), bf16),
+            dma((2 * per,)), dma((2 * per,)), dma((2 * per, 2, 2)), dma((2 * count,)),
+            dma((2 * count, 3)), dma((2 * count, 3)),
+            dma((per, 2)), dma((count,)), dma((2, 2 * count)), dma((2, 2 * count)),
             dma((2, count)), dma((2, count)), dma((2, count)), dma((2, count)),
-            dma((count, m)), dma((count, m)), dma((count,)), dma((m, per)),
+            dma((count, 3)), dma((count, 3)), dma((count,)), dma((m, per)), dma((count, 3)), dma((3,)),
         ],
         compiler_params=pltpu.CompilerParams(
             collective_id=0, has_side_effects=True, vmem_limit_bytes=VMEM_BYTES
         ),
     )(
         layer_input, out_grad, query_weight, key_weight, value_weight,
-        doc_ids.reshape(total, 1), doc_ids.reshape(1, total),
-    )
-
-    def weight_grad(grads):
-        return lax.dot_general(
-            columns, grads, (((0,), (0,)), ((), ())), preferred_element_type=f32
-        )
-
-    return (
-        input_grad,
-        weight_grad(queries_all),
-        weight_grad(pairs_all[0]),
-        weight_grad(pairs_all[1]),
-    )
+        doc_ids.reshape(1, total),
+    )
+
+    step = feats // n
+
+    def whole(array):
+        return pl.BlockSpec(array.shape, lambda i: (0,) * array.ndim)
+
+    def part(rows, width):
+        return pl.BlockSpec((rows, width), lambda i: (i, 0))
+
+    weight_grads = pl.pallas_call(
+        grad_kernel,
+        grid=(n,),
+        out_shape=(
+            jax.ShapeDtypeStruct((tok, feats), bf16),
+            jax.ShapeDtypeStruct((feats, q_cols), f32),
+            jax.ShapeDtypeStruct((feats, pair_width), f32),
+            jax.ShapeDtypeStruct((feats, pair_width), f32),
+        ),
+        in_specs=[part(step, total), whole(queries_all), whole(pairs_all), part(tok // n, feats)],
+        out_specs=(
+            part(tok // n, feats), part(step, q_cols), part(step, pair_width), part(step, pair_width)
+        ),
+        compiler_params=pltpu.CompilerParams(vmem_limit_bytes=VMEM_BYTES),
+    )
+    return weight_grads(turned, queries_all, pairs_all, input_grad)
+
+
+def grad_kernel(xt_ref, dq_ref, kv_ref, in_ref, ig_ref, qg_ref, kg_ref, vg_ref):
+    x = xt_ref[...]
+    qg_ref[...] = jnp.dot(x, dq_ref[...], preferred_element_type=jnp.float32)
+    kg_ref[...] = jnp.dot(x, kv_ref[0], preferred_element_type=jnp.float32)
+    vg_ref[...] = jnp.dot(x, kv_ref[1], preferred_element_type=jnp.float32)
+    ig_ref[...] = in_ref[...]
 
 
 def solution(mesh):
@@ -695,6 +819,6 @@
     n, n_hid, n_rep = mesh.shape["srv"], mesh.shape["hid"], mesh.shape["rep"]
     m = n_hid * n_rep
     inner = body
-    if n == m and n > 2 and n % 2 == 0 and HK == 2 * m and HQ % HK == 0:
+    if n == m and n_hid == 2 and n_rep == 2 and HK == 2 * m and HQ % HK == 0:
         inner = functools.partial(chained, n, n_hid, n_rep)
     return jax.shard_map(inner, mesh=mesh, in_specs=in_specs, out_specs=out_specs, check_vma=False)

time: 164 us -> 142 us (0.87)
  matrix products: 10.2 us -> 0 us
  Pallas kernels: 151 us -> 141 us
  local copies, waits for them, and re-layouts: 2.51 us -> 0 us
    pallas_call x1, Pallas kernels: 151 us -> 133 us  [chained(): pl.pallas_call(functools.partial(chain_kernel, n, m, n_rep, rows, total /...]
    dot_general x3 -> x0, matrix products: 10.2 us -> none  [weight_grad(): lax.dot_general(columns, grads, (((0,), (0,)), ((), ())), preferred_eleme...]
    pallas_call x0 -> x1, Pallas kernels: none -> 7.5 us  [chained(): return weight_grads(turned, queries_all, pairs_all, input_grad)]
    reshape x1 -> x0, local copies, waits for them, and re-layouts: 1.71 us -> none  [chained(): doc_ids.reshape(total, 1)]
where the time goes in v2:
time: 142 us; the launch traced here: 141 us
  Pallas kernels  141 us (99%)
    pallas_call x1, Pallas kernels, chained(): pl.pallas_call(functools.partial(chain_kernel, n, m, n_rep, rows, total /...  133 us
    pallas_call x1, Pallas kernels, chained(): return weight_grads(turned, queries_all, pairs_all, input_grad)  7.5 us

profile of v2, /device:TPU:0, one launch (start us, length us, event | category | flops | bytes accessed | tf_op | source)
XLA Modules:
  0.0 141.5 jit_solution(2197990558164413996)
XLA Ops:
  0.6 133.3 %shard_map.93 = (bf16[1024,1024]{1,0:T(8,128)(2,1)}, bf16[1024,1024]{1,0:T(8,128)(2,1)}, bf16[2,1024,256]{2,1,0:T(8,128)(2,1)}, bf16[256,1024]{1,0:T(8,128)(2,1)}) custom-call(bf16[256,1024]{1,0:T(8,128)(2,1)} %x_ref.1, bf16[256,1024]{1,0:T(8,128)(2,1)} %og_ref.1, bf16[1024,1024]{1,0:T(8,128)(2,1)} %qw_in.1, bf16[1024,256]{1,0:T(8,128)(2,1)} %kw_in.1, ...), custom_call_target="tpu_custom_call" | custom-call | tf_op jit(solution)/shard_map/pallas_call | solution.py:728
  134.0 7.5 %shard_map.94 = (bf16[256,1024]{1,0:T(8,128)(2,1)}, f32[1024,1024]{1,0:T(8,128)}, f32[1024,256]{1,0:T(8,128)}, f32[1024,256]{1,0:T(8,128)}) custom-call(bf16[1024,1024]{1,0:T(8,128)(2,1)} %get-tuple-element.8.xt_ref, bf16[1024,1024]{1,0:T(8,128)(2,1)} %get-tuple-element.9.dq_ref, bf16[2,1024,256]{2,1,0:T(8,128)(2,1)} %get-tuple-element.10.kv_ref, ...), custom_call_target="tpu_custom_call" | custom-call | tf_op jit(solution)/shard_map/pallas_call | solution.py:793

commit v3 on v2

--- a/solution.py
+++ b/solution.py
@@ -264,7 +264,7 @@
     n, m, n_rep, rows, longest,
     x_ref, og_ref, qw_in, kw_in, vw_in, dc_ref,
     turned_out, dqa_out, kva_out, ig_ref,
-    qw_ref, kw_ref, vw_ref, cols_ref, turned, dqa_ref, kva_ref, rs_in, rs_out, og_own, dk, dv, hopped, terms, took, paired, done,
+    qw_ref, kw_ref, vw_ref, cols_ref, turned, dqa_ref, kva_ref, rs_in, rs_out, og_own, dk, dv, hopped, early, terms, took, paired, done,
     h_send, h_recv, a_send, a_recv, b_send, b_recv, og_send, og_recv, rs_send, rs_recv,
     dq_send, dq_recv, kv_send, kv_recv, r_send, r_recv, e_send, e_recv, out_sem, w_sem,
 ):
@@ -275,7 +275,7 @@
     per = tok // rows
     piece = rows // m
     parts = tok // (rows // 2)
-    share = piece // 2
+    share = rows // 4
     q_side = qw_ref.shape[1] // 2
     heads = q_side // DH
     delay = longest // rows
@@ -301,38 +301,45 @@
         return rows_at(j * rows, rows)
 
     def hop_copy(u):
-        src = x_ref.at[rows_at(u * sub + (across // 2) * 2 * share, 2 * share)]
-        return remote(src, hopped.at[u], h_send.at[u], h_recv.at[u], device_at(z, across, n_rep))
-
-    def input_copy(u, i, direct):
+        src = x_ref.at[rows_at(u * sub, sub)]
+        return remote(src, hopped.at[u // 2], h_send, h_recv.at[u // 2], device_at(z, across, n_rep))
+
+    def input_copy(u, i):
         p = (c // 2) * 2 + i
-        plane = c if direct else across
-        if direct:
-            src = x_ref.at[rows_at(u * sub + p * share, share)]
+        plane = across if u % 2 else c
+        if u % 2:
+            src = hopped.at[u // 2, i * share : (i + 1) * share]
         else:
-            src = hopped.at[u, i * share : (i + 1) * share]
-        dst = cols_ref.at[rows_at(z * tok + u * sub + p * share, share)]
+            src = x_ref.at[rows_at(u * sub + i * share, share)]
+        dst = cols_ref.at[rows_at(z * tok + u * sub + i * share, share)]
         copy = remote(
-            src, dst, a_send.at[u, i, int(direct)], a_recv.at[z * parts + u], device_at(plane, p, n_rep)
+            src, dst, a_send.at[u, i], a_recv.at[z * parts + u], device_at(plane, p, n_rep)
         )
         return (plane == z) & (p == c), src, dst, copy
 
-    def send_input(u, i, direct):
-        own, src, dst, copy = input_copy(u, i, direct)
-
-        @pl.when(own)
-        def _():
-            pltpu.make_async_copy(src, dst, a_recv.at[z * parts + u]).start()
-
-        @pl.when(jnp.logical_not(own))
-        def _():
-            copy.start()
+    def send_input(u):
+        for i in range(2):
+            own, src, dst, copy = input_copy(u, i)
+
+            @pl.when(own)
+            def _():
+                pltpu.make_async_copy(src, dst, a_recv.at[z * parts + u]).start()
+
+            @pl.when(jnp.logical_not(own))
+            def _():
+                copy.start()
+
+    def holds(g):
+        return (c // 2 + z // (n // 2) + g) % 2 == 0
+
+    def half_block(g):
+        return cols_ref.at[rows_at(g * sub + (c % 2) * share, share)]
 
     def spread_copy(g, slot):
-        owner, to = ((c, sibling), (c, across), (across, sibling))[slot]
-        block = cols_ref.at[rows_at(g * sub + owner * share, share)]
+        block = half_block(g)
         return remote(
-            block, block, b_send.at[g, slot], b_recv.at[g, slot], device_at(z, to, n_rep)
+            block, block, b_send, b_recv.at[g, slot % 2],
+            device_at(z, across if slot == 1 else sibling, n_rep),
         )
 
     def og_copy(u, s, slot, to):
@@ -348,16 +355,16 @@
     def rs_copy(s, g, to):
         return remote(
             rs_out.at[s, sub_rows(g)], rs_in.at[s, sub_rows(g)],
-            rs_send.at[s, g], rs_recv.at[s, g], device_at(to, c, n_rep),
+            rs_send.at[s], rs_recv.at[s, g], device_at(to, c, n_rep),
         )
 
     def dq_copy(s, j, to):
         block = dqa_ref.at[chunk_rows(j), cols_at(s * q_side, q_side)]
-        return remote(block, block, dq_send.at[s, j], dq_recv.at[s, j], device_at(to, c, n_rep))
+        return remote(block, block, dq_send.at[s], dq_recv.at[s, j], device_at(to, c, n_rep))
 
     def kv_copy(s, j, to):
         block = kva_ref.at[:, chunk_rows(j), cols_at(s * DH, DH)]
-        return remote(block, block, kv_send.at[s, j], kv_recv.at[s, j], device_at(to, c, n_rep))
+        return remote(block, block, kv_send.at[s], kv_recv.at[s, j], device_at(to, c, n_rep))
 
     def term_rows(j, owner):
         return rows_at(j * rows + owner * piece, piece)
@@ -366,14 +373,14 @@
         return remote(
             terms.at[term_rows(j, diagonal if slot else sibling)],
             took.at[slot, rows_at(j * piece, piece)],
-            r_send.at[j, slot], r_recv.at[j, slot], device_at(z, sibling, n_rep),
+            r_send.at[0], r_recv.at[j, slot], device_at(z, sibling, n_rep),
         )
 
     def pair_copy(j):
         block = rows_at(j * piece, piece)
         return remote(
             paired.at[block], took.at[2, block],
-            r_send.at[j, 2], r_recv.at[j, 2], device_at(z, across, n_rep),
+            r_send.at[1], r_recv.at[j, 2], device_at(z, across, n_rep),
         )
 
     def done_place(j):
@@ -386,14 +393,27 @@
         )
 
     def spread(g):
-        block = cols_ref.at[rows_at(g * sub + c * share, share)]
-        pltpu.make_async_copy(block, block, a_recv.at[g]).wait()
-        for slot in (1, 0):
-            spread_copy(g, slot).start()
-
-    def relay(j):
-        spread_copy(j, 1).wait_recv()
-        spread_copy(j, 2).start()
+        @pl.when(holds(g))
+        def _():
+            block = half_block(g)
+            pltpu.make_async_copy(block, block, a_recv.at[g]).wait()
+            for slot in (1, 0):
+                spread_copy(g, slot).start()
+
+    def relay(g):
+        @pl.when(jnp.logical_not(holds(g)))
+        def _():
+            spread_copy(g, 1).wait_recv()
+            spread_copy(g, 2).start()
+
+    def await_input(g):
+        @pl.when(holds(g))
+        def _():
+            spread_copy(g, 0).wait_recv()
+
+        @pl.when(jnp.logical_not(holds(g)))
+        def _():
+            spread_copy(g, 2).wait_recv()
 
     def project(s, g):
         x = cols_ref[sub_rows(g), :]
@@ -418,11 +438,10 @@
             src, dst = dqa_ref.at[chunk_rows(j)], dqa_out.at[chunk_rows(j)]
         else:
             src, dst = turned.at[:, chunk_rows(j)], turned_out.at[:, chunk_rows(j)]
-        return pltpu.make_async_copy(src, dst, out_sem.at[j, slot])
+        return pltpu.make_async_copy(src, dst, out_sem.at[slot])
 
     def reduce_a(g):
-        for slot in (0, 2):
-            spread_copy(g, slot).wait_recv()
+        await_input(g)
 
         @pl.when(is_end)
         def _():
@@ -505,9 +524,7 @@
         for slot in (1, 2):
             out_copy(j, slot).start()
         flip = (((1,), (1,)), ((), ()))
-        value = lax.dot_general(
-            dqa_ref[chunk_rows(j), :], qw_ref[...], flip, preferred_element_type=f32
-        )
+        value = early[chunk_rows(j), :]
         value = value + lax.dot_general(
             kva_ref[0, chunk_rows(j), :], kw_ref[...], flip, preferred_element_type=f32
         )
@@ -518,13 +535,9 @@
         for slot in (1, 0):
             term_copy(j, slot).start()
 
-        @pl.when(j > 0)
-        def _():
-            combine(j - 1)
-
         @pl.when(j > 1)
         def _():
-            finish(j - 2)
+            combine(j - 2)
 
     def pass_b(v):
         @pl.when(v < count)
@@ -545,6 +558,11 @@
             @pl.when(not_end)
             def _():
                 dq_copy(side_a, v, outer).start()
+
+            early[chunk_rows(v), :] = lax.dot_general(
+                dqa_ref[chunk_rows(v), :], qw_ref[...], (((1,), (1,)), ((), ())),
+                preferred_element_type=f32,
+            )
 
         @pl.when(v >= delay)
         def _():
@@ -564,12 +582,7 @@
     for copy in loads:
         copy.start()
     greet(n, m, n_rep)
-    for u in range(parts):
-        hop_copy(u).start()
-    for u in range(parts):
-        for i in range(2):
-            send_input(u, i, True)
-
+    send_input(0)
     @pl.when(is_end)
     def _():
         dk[...] = jnp.zeros_like(dk)
@@ -577,8 +590,7 @@
 
     def forward(u):
         hop_copy(u).wait_recv()
-        for i in range(2):
-            send_input(u, i, False)
+        send_input(u)
 
     def send_og(u, slot):
         to = (far_end, near_end)[slot]
@@ -594,39 +606,43 @@
             def _():
                 copy.start()
 
-    forward(0)
-    forward(1)
+    def begin():
+        for u in range(1, lead):
+            if u < parts and u % 2:
+                forward(u)
+            spread(u)
+        relay(1)
+        for u in range(per):
+            send_og(u, 1)
+
     spread(0)
-    for u in range(2, parts):
-        forward(u)
-    for g in range(1, lead):
-        spread(g)
-    for g in range(2):
-        relay(g)
-    for u in range(per):
-        send_og(u, 1)
-
-        @pl.when(not_end)
-        def _():
-            send_og(u, 0)
+    for u in range(1, parts, 2):
+        hop_copy(u).start()
+    for u in range(2, parts, 2):
+        send_input(u)
     for copy in loads:
         copy.wait()
+    relay(0)
 
     def step(k, carry):
         even = k % 2 == 0
         j = k // 2
 
-        @pl.when(is_end & even & (j > 0) & (j <= per))
-        def _():
-            send_og(j - 1, 0)
-
-        @pl.when(k + 2 < 2 * count)
-        def _():
-            relay(k + 2)
+        @pl.when((k % 2 == 1) & (j >= z * per) & (j < z * per + per))
+        def _():
+            send_og(j - z * per, 0)
+
+        @pl.when((k > 0) & (k + 1 < 2 * count))
+        def _():
+            relay(k + 1)
 
         @pl.when((k >= 2 * e) & (k < 2 * e + 2 * count))
         def _():
             reduce_a(k - 2 * e)
+
+        @pl.when(k == 0)
+        def _():
+            begin()
 
         @pl.when(k + lead < 2 * count)
         def _():
@@ -658,47 +674,50 @@
         return carry
 
     lax.fori_loop(0, 2 * (count + delay + 2 * (n - 1) + 1), step, 0)
-    combine(jnp.int32(count - 1))
-    finish(jnp.int32(count - 2))
-    finish(jnp.int32(count - 1))
+    for j in (count - 2, count - 1):
+        combine(jnp.int32(j))
+
+    def close(j, carry):
+        finish(j)
+        return carry
+
+    lax.fori_loop(0, count, close, 0)
+
+    def settled(ref, sem):
+        pltpu.make_async_copy(ref, ref, sem).wait()
 
     def drain(j, carry):
-        for slot in range(3):
-            spread_copy(2 * j, slot).wait_send()
-            spread_copy(2 * j + 1, slot).wait_send()
-        for slot in range(2):
-            term_copy(j, slot).wait_send()
-        pair_copy(j).wait_send()
+        @pl.when(jnp.logical_not((j // per == z) & (c == z)))
+        def _():
+            done_copy(j).wait_send()
+
+        return carry
+
+    settled(cols_ref.at[: 3 * total // m], b_send)
+    settled(terms.at[: 2 * total // m], r_send.at[0])
+    settled(paired, r_send.at[1])
+    settled(turned, out_sem.at[0])
+    settled(dqa_ref, out_sem.at[1])
+    settled(kva_ref, out_sem.at[2])
+    settled(rs_out.at[side_a], rs_send.at[side_a])
+    settled(og_own, dq_send.at[side_b])
+    settled(kva_ref.at[side_b], kv_send.at[side_b])
+
+    @pl.when(not_end)
+    def _():
+        settled(rs_out.at[side_b], rs_send.at[side_b])
+        settled(og_own, dq_send.at[side_a])
+        settled(kva_ref.at[side_a], kv_send.at[side_a])
+
+    lax.fori_loop(0, count, drain, 0)
+    settled(hopped, h_send)
+    for u in range(parts):
         for i in range(2):
-            rs_copy(side_a, 2 * j + i, inner).wait_send()
-        for slot in range(3):
-            out_copy(j, slot).wait()
-        dq_copy(side_b, j, inner).wait_send()
-        kv_copy(side_b, j, inner).wait_send()
-
-        @pl.when(not_end)
-        def _():
-            for i in range(2):
-                rs_copy(side_b, 2 * j + i, outer).wait_send()
-            dq_copy(side_a, j, outer).wait_send()
-            kv_copy(side_a, j, outer).wait_send()
-
-        @pl.when(jnp.logical_not((j // per == z) & (c == z)))
-        def _():
-            done_copy(j).wait_send()
-
-        return carry
-
-    lax.fori_loop(0, count, drain, 0)
-    for u in range(parts):
-        hop_copy(u).wait_send()
-        for i in range(2):
-            for direct in (True, False):
-                own, _, _, copy = input_copy(u, i, direct)
-
-                @pl.when(jnp.logical_not(own))
-                def _():
-                    copy.wait_send()
+            own, _, _, copy = input_copy(u, i)
+
+            @pl.when(jnp.logical_not(own))
+            def _():
+                copy.wait_send()
     for u in range(per):
         _, _, copy = og_copy(u, side_a, 0, far_end)
         copy.wait_send()
@@ -748,16 +767,17 @@
             pltpu.VMEM((total, q_cols // 2), bf16),
             pltpu.VMEM((total, DH), f32),
             pltpu.VMEM((total, DH), f32),
-            pltpu.VMEM((2 * per, rows // 4, feats), bf16),
+            pltpu.VMEM((per, rows // 2, feats), bf16),
+            pltpu.VMEM((total, feats), f32),
             pltpu.VMEM((total, feats), bf16),
             pltpu.VMEM((3, count * piece, feats), bf16),
             pltpu.VMEM((count * piece, feats), bf16),
             pltpu.VMEM((count * piece, feats), bf16),
-            dma((2 * per,)), dma((2 * per,)), dma((2 * per, 2, 2)), dma((2 * count,)),
-            dma((2 * count, 3)), dma((2 * count, 3)),
-            dma((per, 2)), dma((count,)), dma((2, 2 * count)), dma((2, 2 * count)),
-            dma((2, count)), dma((2, count)), dma((2, count)), dma((2, count)),
-            dma((count, 3)), dma((count, 3)), dma((count,)), dma((m, per)), dma((count, 3)), dma((3,)),
+            dma, dma((per,)), dma((2 * per, 2)), dma((2 * count,)),
+            dma, dma((2 * count, 2)),
+            dma((per, 2)), dma((count,)), dma((2,)), dma((2, 2 * count)),
+            dma((2,)), dma((2, count)), dma((2,)), dma((2, count)),
+            dma((2,)), dma((count, 3)), dma((count,)), dma((m, per)), dma((3,)), dma((3,)),
         ],
         compiler_params=pltpu.CompilerParams(
             collective_id=0, has_side_effects=True, vmem_limit_bytes=VMEM_BYTES

time: 142 us -> 140 us (0.986)
  Pallas kernels: 141 us -> 139 us
    pallas_call x1, Pallas kernels: 133 us -> 131 us  [chained(): pl.pallas_call(functools.partial(chain_kernel, n, m, n_rep, rows, total /...]
where the time goes in v3:
time: 140 us; the launch traced here: 139 us
  Pallas kernels  139 us (99%)
    pallas_call x1, Pallas kernels, chained(): pl.pallas_call(functools.partial(chain_kernel, n, m, n_rep, rows, total /...  131 us
    pallas_call x1, Pallas kernels, chained(): return weight_grads(turned, queries_all, pairs_all, input_grad)  7.5 us

profile of v3, /device:TPU:0, one launch (start us, length us, event | category | flops | bytes accessed | tf_op | source)
XLA Modules:
  0.0 139.3 jit_solution(3438004411389342249)
XLA Ops:
  0.6 131.2 %shard_map.93 = (bf16[1024,1024]{1,0:T(8,128)(2,1)}, bf16[1024,1024]{1,0:T(8,128)(2,1)}, bf16[2,1024,256]{2,1,0:T(8,128)(2,1)}, bf16[256,1024]{1,0:T(8,128)(2,1)}) custom-call(bf16[256,1024]{1,0:T(8,128)(2,1)} %x_ref.1, bf16[256,1024]{1,0:T(8,128)(2,1)} %og_ref.1, bf16[1024,1024]{1,0:T(8,128)(2,1)} %qw_in.1, bf16[1024,256]{1,0:T(8,128)(2,1)} %kw_in.1, ...), custom_call_target="tpu_custom_call" | custom-call | tf_op jit(solution)/shard_map/pallas_call | solution.py:747
  131.8 7.5 %shard_map.94 = (bf16[256,1024]{1,0:T(8,128)(2,1)}, f32[1024,1024]{1,0:T(8,128)}, f32[1024,256]{1,0:T(8,128)}, f32[1024,256]{1,0:T(8,128)}) custom-call(bf16[1024,1024]{1,0:T(8,128)(2,1)} %get-tuple-element.8.xt_ref, bf16[1024,1024]{1,0:T(8,128)(2,1)} %get-tuple-element.9.dq_ref, bf16[2,1024,256]{2,1,0:T(8,128)(2,1)} %get-tuple-element.10.kv_ref, ...), custom_call_target="tpu_custom_call" | custom-call | tf_op jit(solution)/shard_map/pallas_call | solution.py:813

commit v4 on v3

--- a/solution.py
+++ b/solution.py
@@ -535,9 +535,9 @@
         for slot in (1, 0):
             term_copy(j, slot).start()
 
-        @pl.when(j > 1)
-        def _():
-            combine(j - 2)
+        @pl.when(j > 0)
+        def _():
+            combine(j - 1)
 
     def pass_b(v):
         @pl.when(v < count)
@@ -615,6 +615,8 @@
         for u in range(per):
             send_og(u, 1)
 
+            send_og(u, 0)
+
     spread(0)
     for u in range(1, parts, 2):
         hop_copy(u).start()
@@ -628,9 +630,6 @@
         even = k % 2 == 0
         j = k // 2
 
-        @pl.when((k % 2 == 1) & (j >= z * per) & (j < z * per + per))
-        def _():
-            send_og(j - z * per, 0)
 
         @pl.when((k > 0) & (k + 1 < 2 * count))
         def _():
@@ -674,7 +673,7 @@
         return carry
 
     lax.fori_loop(0, 2 * (count + delay + 2 * (n - 1) + 1), step, 0)
-    for j in (count - 2, count - 1):
+    for j in (count - 1,):
         combine(jnp.int32(j))
 
     def close(j, carry):
@@ -787,7 +786,8 @@
         doc_ids.reshape(1, total),
     )
 
-    step = feats // n
+    blocks = n // 2
+    step = feats // blocks
 
     def whole(array):
         return pl.BlockSpec(array.shape, lambda i: (0,) * array.ndim)
@@ -797,16 +797,16 @@
 
     weight_grads = pl.pallas_call(
         grad_kernel,
-        grid=(n,),
+        grid=(blocks,),
         out_shape=(
             jax.ShapeDtypeStruct((tok, feats), bf16),
             jax.ShapeDtypeStruct((feats, q_cols), f32),
             jax.ShapeDtypeStruct((feats, pair_width), f32),
             jax.ShapeDtypeStruct((feats, pair_width), f32),
         ),
-        in_specs=[part(step, total), whole(queries_all), whole(pairs_all), part(tok // n, feats)],
+        in_specs=[part(step, total), whole(queries_all), whole(pairs_all), part(tok // blocks, feats)],
         out_specs=(
-            part(tok // n, feats), part(step, q_cols), part(step, pair_width), part(step, pair_width)
+            part(tok // blocks, feats), part(step, q_cols), part(step, pair_width), part(step, pair_width)
         ),
         compiler_params=pltpu.CompilerParams(vmem_limit_bytes=VMEM_BYTES),
     )

time: 140 us -> 135 us (0.964)
  Pallas kernels: 139 us -> 134 us
    pallas_call x1, Pallas kernels: 131 us -> 127 us  [chained(): pl.pallas_call(functools.partial(chain_kernel, n, m, n_rep, rows, total /...]
where the time goes in v4:
time: 135 us; the launch traced here: 134 us
  Pallas kernels  134 us (99%)
    pallas_call x1, Pallas kernels, chained(): pl.pallas_call(functools.partial(chain_kernel, n, m, n_rep, rows, total /...  127 us
    pallas_call x1, Pallas kernels, chained(): return weight_grads(turned, queries_all, pairs_all, input_grad)  7.18 us

profile of v4, /device:TPU:0, one launch (start us, length us, event | category | flops | bytes accessed | tf_op | source)
XLA Modules:
  0.0 134.3 jit_solution(396455927237758126)
XLA Ops:
  0.6 126.5 %shard_map.93 = (bf16[1024,1024]{1,0:T(8,128)(2,1)}, bf16[1024,1024]{1,0:T(8,128)(2,1)}, bf16[2,1024,256]{2,1,0:T(8,128)(2,1)}, bf16[256,1024]{1,0:T(8,128)(2,1)}) custom-call(bf16[256,1024]{1,0:T(8,128)(2,1)} %x_ref.1, bf16[256,1024]{1,0:T(8,128)(2,1)} %og_ref.1, bf16[1024,1024]{1,0:T(8,128)(2,1)} %qw_in.1, bf16[1024,256]{1,0:T(8,128)(2,1)} %kw_in.1, ...), custom_call_target="tpu_custom_call" | custom-call | tf_op jit(solution)/shard_map/pallas_call | solution.py:746
  127.2 7.2 %shard_map.94 = (bf16[256,1024]{1,0:T(8,128)(2,1)}, f32[1024,1024]{1,0:T(8,128)}, f32[1024,256]{1,0:T(8,128)}, f32[1024,256]{1,0:T(8,128)}) custom-call(bf16[1024,1024]{1,0:T(8,128)(2,1)} %get-tuple-element.8.xt_ref, bf16[1024,1024]{1,0:T(8,128)(2,1)} %get-tuple-element.9.dq_ref, bf16[2,1024,256]{2,1,0:T(8,128)(2,1)} %get-tuple-element.10.kv_ref, ...), custom_call_target="tpu_custom_call" | custom-call | tf_op jit(solution)/shard_map/pallas_call | solution.py:813

commit v5 on v4

--- a/solution.py
+++ b/solution.py
@@ -262,9 +262,9 @@
 
 def chain_kernel(
     n, m, n_rep, rows, longest,
-    x_ref, og_ref, qw_in, kw_in, vw_in, dc_ref,
+    x_ref, og_ref, qw_in, kw_in, vw_in, dc_in,
     turned_out, dqa_out, kva_out, ig_ref,
-    qw_ref, kw_ref, vw_ref, cols_ref, turned, dqa_ref, kva_ref, rs_in, rs_out, og_own, dk, dv, hopped, early, terms, took, paired, done,
+    qw_ref, kw_ref, vw_ref, dc_ref, cols_ref, turned, dqa_ref, kva_ref, rs_in, rs_out, og_own, dk, dv, hopped, early, terms, took, paired, done,
     h_send, h_recv, a_send, a_recv, b_send, b_recv, og_send, og_recv, rs_send, rs_recv,
     dq_send, dq_recv, kv_send, kv_recv, r_send, r_recv, e_send, e_recv, out_sem, w_sem,
 ):
@@ -578,6 +578,7 @@
         pltpu.make_async_copy(qw_in, qw_ref, w_sem.at[0]),
         pltpu.make_async_copy(kw_in, kw_ref, w_sem.at[1]),
         pltpu.make_async_copy(vw_in, vw_ref, w_sem.at[2]),
+        pltpu.make_async_copy(dc_in, dc_ref, w_sem.at[3]),
     ]
     for copy in loads:
         copy.start()
@@ -743,6 +744,13 @@
     width = q_cols // 2 + pair_width
     dma = pltpu.SemaphoreType.DMA
     ANY = pl.BlockSpec(memory_space=pl.ANY)
+    HBM = pl.BlockSpec(memory_space=pltpu.HBM)
+    held = [
+        pltpu.with_memory_space_constraint(array, pltpu.HBM)
+        for array in (
+            layer_input, out_grad, query_weight, key_weight, value_weight, doc_ids.reshape(1, total)
+        )
+    ]
     turned, queries_all, pairs_all, input_grad = pl.pallas_call(
         functools.partial(chain_kernel, n, m, n_rep, rows, total // 2),
         out_shape=(
@@ -751,12 +759,13 @@
             jax.ShapeDtypeStruct((2, total, pair_width), bf16),
             jax.ShapeDtypeStruct((tok, feats), bf16),
         ),
-        in_specs=[ANY] * 5 + [VM],
+        in_specs=[HBM] * 6,
         out_specs=(ANY,) * 4,
         scratch_shapes=[
             pltpu.VMEM(query_weight.shape, bf16),
             pltpu.VMEM(key_weight.shape, bf16),
             pltpu.VMEM(value_weight.shape, bf16),
+            pltpu.VMEM((1, total), jnp.int32),
             pltpu.VMEM((total, feats), bf16),
             pltpu.VMEM((feats, total), bf16),
             pltpu.VMEM((total, q_cols), bf16),
@@ -776,49 +785,57 @@
             dma, dma((2 * count, 2)),
             dma((per, 2)), dma((count,)), dma((2,)), dma((2, 2 * count)),
             dma((2,)), dma((2, count)), dma((2,)), dma((2, count)),
-            dma((2,)), dma((count, 3)), dma((count,)), dma((m, per)), dma((3,)), dma((3,)),
+            dma((2,)), dma((count, 3)), dma((count,)), dma((m, per)), dma((3,)), dma((4,)),
         ],
         compiler_params=pltpu.CompilerParams(
-            collective_id=0, has_side_effects=True, vmem_limit_bytes=VMEM_BYTES
+            collective_id=0, has_side_effects=True, vmem_limit_bytes=44 * 1024 * 1024
         ),
     )(
-        layer_input, out_grad, query_weight, key_weight, value_weight,
-        doc_ids.reshape(1, total),
-    )
-
-    blocks = n // 2
-    step = feats // blocks
-
-    def whole(array):
-        return pl.BlockSpec(array.shape, lambda i: (0,) * array.ndim)
-
-    def part(rows, width):
-        return pl.BlockSpec((rows, width), lambda i: (i, 0))
-
+        *held
+    )
+
+    blocks = n
     weight_grads = pl.pallas_call(
-        grad_kernel,
-        grid=(blocks,),
+        functools.partial(grad_kernel, blocks),
         out_shape=(
             jax.ShapeDtypeStruct((tok, feats), bf16),
             jax.ShapeDtypeStruct((feats, q_cols), f32),
             jax.ShapeDtypeStruct((feats, pair_width), f32),
             jax.ShapeDtypeStruct((feats, pair_width), f32),
         ),
-        in_specs=[part(step, total), whole(queries_all), whole(pairs_all), part(tok // blocks, feats)],
-        out_specs=(
-            part(tok // blocks, feats), part(step, q_cols), part(step, pair_width), part(step, pair_width)
-        ),
-        compiler_params=pltpu.CompilerParams(vmem_limit_bytes=VMEM_BYTES),
+        in_specs=[VM] * 4,
+        out_specs=(HBM,) * 4,
+        scratch_shapes=[
+            pltpu.VMEM((feats, q_cols), f32),
+            pltpu.VMEM((feats, pair_width), f32),
+            pltpu.VMEM((feats, pair_width), f32),
+            dma((blocks, 3)), dma,
+        ],
+        compiler_params=pltpu.CompilerParams(vmem_limit_bytes=32 * 1024 * 1024),
     )
     return weight_grads(turned, queries_all, pairs_all, input_grad)
 
 
-def grad_kernel(xt_ref, dq_ref, kv_ref, in_ref, ig_ref, qg_ref, kg_ref, vg_ref):
-    x = xt_ref[...]
-    qg_ref[...] = jnp.dot(x, dq_ref[...], preferred_element_type=jnp.float32)
-    kg_ref[...] = jnp.dot(x, kv_ref[0], preferred_element_type=jnp.float32)
-    vg_ref[...] = jnp.dot(x, kv_ref[1], preferred_element_type=jnp.float32)
-    ig_ref[...] = in_ref[...]
+def grad_kernel(
+    blocks, xt_ref, dq_ref, kv_ref, in_ref, ig_out, qg_out, kg_out, vg_out, qg, kg, vg, sems, sem
+):
+    whole = pltpu.make_async_copy(in_ref, ig_out, sem)
+    whole.start()
+    copies = []
+    step = xt_ref.shape[0] // blocks
+    for b in range(blocks):
+        rows = slice(b * step, (b + 1) * step)
+        x = xt_ref[rows, :]
+        for i, (grads, held, out) in enumerate(
+            ((dq_ref, qg, qg_out), (kv_ref.at[0], kg, kg_out), (kv_ref.at[1], vg, vg_out))
+        ):
+            held[rows, :] = jnp.dot(x, grads[...], preferred_element_type=jnp.float32)
+            copy = pltpu.make_async_copy(held.at[rows], out.at[rows], sems.at[b, i])
+            copy.start()
+            copies.append(copy)
+    for copy in copies:
+        copy.wait()
+    whole.wait()
 
 
 def solution(mesh):

time: 135 us -> 131 us (0.970)
  Pallas kernels: 134 us -> 130 us
    pallas_call x1, Pallas kernels: 7.18 us -> 4.37 us  [chained(): return weight_grads(turned, queries_all, pairs_all, input_grad)]
where the time goes in v5:
time: 131 us
  Pallas kernels  130 us (99%)
    pallas_call x1, Pallas kernels, chained(): pl.pallas_call(functools.partial(chain_kernel, n, m, n_rep, rows, total /...  126 us
    pallas_call x1, Pallas kernels, chained(): return weight_grads(turned, queries_all, pairs_all, input_grad)  4.37 us

profile of v5, /device:TPU:0, one launch (start us, length us, event | category | flops | bytes accessed | tf_op | source)
XLA Modules:
  0.0 131.1 jit_solution(11659743955361671523)
XLA Ops:
  0.6 126.1 %shard_map.93 = (bf16[1024,1024]{1,0:T(8,128)(2,1)S(1)}, bf16[1024,1024]{1,0:T(8,128)(2,1)S(1)}, bf16[2,1024,256]{2,1,0:T(8,128)(2,1)S(1)}, bf16[256,1024]{1,0:T(8,128)(2,1)S(1)}) custom-call(bf16[256,1024]{1,0:T(8,128)(2,1)} %x_ref.1, bf16[256,1024]{1,0:T(8,128)(2,1)} %og_ref.1, bf16[1024,1024]{1,0:T(8,128)(2,1)} %qw_in.1, bf16[1024,256]{1,0:T(8,128)(2,1)} %kw_in.1, ...), custom_call_target="tpu_custom_call" | custom-call | tf_op jit(solution)/shard_map/pallas_call | solution.py:754
  126.7 4.4 %shard_map.94 = (bf16[256,1024]{1,0:T(8,128)(2,1)}, f32[1024,1024]{1,0:T(8,128)}, f32[1024,256]{1,0:T(8,128)}, f32[1024,256]{1,0:T(8,128)}) custom-call(bf16[1024,1024]{1,0:T(8,128)(2,1)S(1)} %get-tuple-element.8.xt_ref, bf16[1024,1024]{1,0:T(8,128)(2,1)S(1)} %get-tuple-element.9.dq_ref, bf16[2,1024,256]{2,1,0:T(8,128)(2,1)S(1)} %get-tuple-element.10.kv_ref, ...), custom_call_target="tpu_custom_call" | custom-call | tf_op jit(solution)/shard_map/pallas_call | solution.py:816

commit v6 on v5

--- a/solution.py
+++ b/solution.py
@@ -313,7 +313,7 @@
             src = x_ref.at[rows_at(u * sub + i * share, share)]
         dst = cols_ref.at[rows_at(z * tok + u * sub + i * share, share)]
         copy = remote(
-            src, dst, a_send.at[u, i], a_recv.at[z * parts + u], device_at(plane, p, n_rep)
+            src, dst, a_send.at[u, i], a_recv.at[(z * parts + u) // 2], device_at(plane, p, n_rep)
         )
         return (plane == z) & (p == c), src, dst, copy
 
@@ -323,7 +323,7 @@
 
             @pl.when(own)
             def _():
-                pltpu.make_async_copy(src, dst, a_recv.at[z * parts + u]).start()
+                pltpu.make_async_copy(src, dst, a_recv.at[(z * parts + u) // 2]).start()
 
             @pl.when(jnp.logical_not(own))
             def _():
@@ -396,7 +396,7 @@
         @pl.when(holds(g))
         def _():
             block = half_block(g)
-            pltpu.make_async_copy(block, block, a_recv.at[g]).wait()
+            pltpu.make_async_copy(block, block, a_recv.at[g // 2]).wait()
             for slot in (1, 0):
                 spread_copy(g, slot).start()
 
@@ -612,11 +612,14 @@
             if u < parts and u % 2:
                 forward(u)
             spread(u)
-        relay(1)
+        @pl.when(is_end)
+        def _():
+            relay(1)
+
+        for u in range(per):
+            send_og(u, 0)
         for u in range(per):
             send_og(u, 1)
-
-            send_og(u, 0)
 
     spread(0)
     for u in range(1, parts, 2):
@@ -632,9 +635,9 @@
         j = k // 2
 
 
-        @pl.when((k > 0) & (k + 1 < 2 * count))
-        def _():
-            relay(k + 1)
+        @pl.when((k > 0) & (k + 1 - e < 2 * count) & (k + 1 - e > 0))
+        def _():
+            relay(k + 1 - e)
 
         @pl.when((k >= 2 * e) & (k < 2 * e + 2 * count))
         def _():
@@ -781,7 +784,7 @@
             pltpu.VMEM((3, count * piece, feats), bf16),
             pltpu.VMEM((count * piece, feats), bf16),
             pltpu.VMEM((count * piece, feats), bf16),
-            dma, dma((per,)), dma((2 * per, 2)), dma((2 * count,)),
+            dma, dma((per,)), dma((2 * per, 2)), dma((count,)),
             dma, dma((2 * count, 2)),
             dma((per, 2)), dma((count,)), dma((2,)), dma((2, 2 * count)),
             dma((2,)), dma((2, count)), dma((2,)), dma((2, count)),

time: 131 us -> 131 us (level)
  no operation moved by 1% of the time
where the time goes in v6:
time: 131 us
  Pallas kernels  130 us (99%)
    pallas_call x1, Pallas kernels, chained(): pl.pallas_call(functools.partial(chain_kernel, n, m, n_rep, rows, total /...  126 us
    pallas_call x1, Pallas kernels, chained(): return weight_grads(turned, queries_all, pairs_all, input_grad)  4.37 us

profile of v6, /device:TPU:0, one launch (start us, length us, event | category | flops | bytes accessed | tf_op | source)
XLA Modules:
  0.0 131.0 jit_solution(8240479530871997550)
XLA Ops:
  0.6 126.0 %shard_map.93 = (bf16[1024,1024]{1,0:T(8,128)(2,1)S(1)}, bf16[1024,1024]{1,0:T(8,128)(2,1)S(1)}, bf16[2,1024,256]{2,1,0:T(8,128)(2,1)S(1)}, bf16[256,1024]{1,0:T(8,128)(2,1)S(1)}) custom-call(bf16[256,1024]{1,0:T(8,128)(2,1)} %x_ref.1, bf16[256,1024]{1,0:T(8,128)(2,1)} %og_ref.1, bf16[1024,1024]{1,0:T(8,128)(2,1)} %qw_in.1, bf16[1024,256]{1,0:T(8,128)(2,1)} %kw_in.1, ...), custom_call_target="tpu_custom_call" | custom-call | tf_op jit(solution)/shard_map/pallas_call | solution.py:757
  126.6 4.4 %shard_map.94 = (bf16[256,1024]{1,0:T(8,128)(2,1)}, f32[1024,1024]{1,0:T(8,128)}, f32[1024,256]{1,0:T(8,128)}, f32[1024,256]{1,0:T(8,128)}) custom-call(bf16[1024,1024]{1,0:T(8,128)(2,1)S(1)} %get-tuple-element.8.xt_ref, bf16[1024,1024]{1,0:T(8,128)(2,1)S(1)} %get-tuple-element.9.dq_ref, bf16[2,1024,256]{2,1,0:T(8,128)(2,1)S(1)} %get-tuple-element.10.kv_ref, ...), custom_call_target="tpu_custom_call" | custom-call | tf_op jit(solution)/shard_map/pallas_call | solution.py:819
